TPU v7x, 256 devices: a whole 4x4x8 slice. The times are simulated.
256 devices in a mesh: head: 8 (over y, core), ctx: 32 (over z, x).
Axes of the slice: x: 4, y: 4, z: 8, core: 2. Of those that a mesh axis runs over, the one named last changes fastest.
Arguments:
- queries: bfloat16 [24576, 8192], P(('ctx', 'head')), may hold values from -6 to 6
- keys: bfloat16 [24576, 8192], P(('ctx', 'head')), may hold values from -6 to 6
- values: bfloat16 [24576, 8192], P(('ctx', 'head')), may hold values from -6 to 6
- pattern: int32 [3, 32, 6, 6], P(None, 'ctx'), may hold values 0 or 1
Outputs:
- attended: bfloat16 [24576, 8192], P(('ctx', 'head'))
All inputs are finite; a program needn't handle non-finite values. No bound on the sum of `pattern` on one device may be relied on, other than what follows from the above.
Results may differ from a plain program's by a relative error of at most 0.009.
Values may be sent and summed in bfloat16 or wider, within the bound.
No kernel may reach another device: no remote copies, remote signals or barrier semaphores. Data moves between devices by JAX's collectives and lax.ppermute only.
A program may use at most 128 MiB of HBM per device.

v0:
```python
import jax
import jax.numpy as jnp
from jax import lax
from jax.sharding import PartitionSpec as P

H = 64
HD = 128
BLOCK = 128
C = 768


masked_score = -1e30


def from_behind(value, axis, steps):
    count = lax.axis_size(axis)
    leading, last = (max(0, -steps), min(count, count - steps))
    return lax.ppermute(value, axis, [(source, source + steps) for source in range(leading, last)])


def block_allow(block_flags, block_size):
    blocks = block_flags.shape[0]
    tiled = jnp.broadcast_to(
        block_flags[:, None, :, None], (blocks, block_size, blocks, block_size)
    )
    return tiled.reshape(blocks * block_size, blocks * block_size) > 0


def partial_block(head_queries, head_keys, head_values, allowed):
    scaling = head_queries.shape[2] ** (-0.5)
    scores = (
        jnp.einsum("qhd,khd->hqk", head_queries, head_keys, preferred_element_type=jnp.float32)
        * scaling
    )
    scores = jnp.where(allowed[None], scores, masked_score)
    maxima = jnp.max(scores, axis=2)
    expo = jnp.where(allowed[None], jnp.exp(scores - maxima[:, :, None]), 0.0)
    totals = jnp.sum(expo, axis=2)
    mixture = jnp.einsum(
        "hqk,khd->qhd", expo.astype(jnp.bfloat16), head_values, preferred_element_type=jnp.float32
    )
    return (mixture, maxima, totals)


def empty_block(head_queries):
    rows, heads, depth = head_queries.shape
    mixture = jnp.zeros((rows, heads, depth), jnp.float32)
    maxima = jnp.full((heads, rows), masked_score, jnp.float32)
    totals = jnp.zeros((heads, rows), jnp.float32)
    return (mixture, maxima, totals)


def guarded_block(live, head_queries, head_keys, head_values, allowed):

    def active(operands):
        return partial_block(operands[0], operands[1], operands[2], operands[3])

    def skipped(operands):
        return empty_block(operands[0])

    return lax.cond(live, active, skipped, (head_queries, head_keys, head_values, allowed))


def keys_route(head_queries, head_keys, head_values, block_flags, distance, position):
    far_keys, far_values = from_behind((head_keys, head_values), "ctx", distance)
    allowed = block_allow(block_flags, BLOCK)
    return guarded_block(position >= distance, head_queries, far_keys, far_values, allowed)


def regroup(array, groups):
    return array.reshape(array.shape[0], groups, array.shape[1] // groups)


def body(queries, keys, values, pattern):
    groups = lax.axis_size("head")
    span_count = lax.axis_size("ctx")
    position = lax.axis_index("ctx")
    far = span_count // 2
    local_heads = H // groups
    tok_rows, width = queries.shape
    moved = (
        lax.all_to_all(regroup(queries, groups), "head", split_axis=1, concat_axis=0, tiled=True),
        lax.all_to_all(regroup(keys, groups), "head", split_axis=1, concat_axis=0, tiled=True),
        lax.all_to_all(regroup(values, groups), "head", split_axis=1, concat_axis=0, tiled=True),
    )
    head_queries = moved[0].reshape(C, local_heads, HD)
    head_keys = moved[1].reshape(C, local_heads, HD)
    head_values = moved[2].reshape(C, local_heads, HD)
    own_flags = pattern[:, 0]
    span_rows = lax.iota(jnp.int32, C)
    causal = span_rows[:, None] >= span_rows[None, :]
    partials = [partial_block(head_queries, head_keys, head_values, causal)]
    for number, distance in enumerate((far - 1, far)):
        partials.append(
            keys_route(head_queries, head_keys, head_values, own_flags[number], distance, position)
        )
    farthest = far + 1
    partials.append(
        keys_route(head_queries, head_keys, head_values, own_flags[2], farthest, position)
    )
    cleaned = [
        (mixture, jnp.where(totals > 0.0, maxima, masked_score), totals)
        for mixture, maxima, totals in partials
    ]
    highest = cleaned[0][1]
    for entry in cleaned[1:]:
        highest = jnp.maximum(highest, entry[1])
    numerator = jnp.zeros((C, local_heads, HD), jnp.float32)
    denominator = jnp.zeros((local_heads, C), jnp.float32)
    for mixture, maxima, totals in cleaned:
        factor = jnp.exp(maxima - highest)
        numerator = numerator + factor.T[:, :, None] * mixture
        denominator = denominator + factor * totals
    combined = (numerator / denominator.T[:, :, None]).astype(jnp.bfloat16)
    returned = lax.all_to_all(
        combined.reshape(C, 1, local_heads * HD), "head", split_axis=0, concat_axis=1, tiled=True
    )
    return returned.reshape(tok_rows, width)


def solution(mesh):
    placed = (
        P(("ctx", "head"), None),
        P(("ctx", "head"), None),
        P(("ctx", "head"), None),
        P(None, "ctx", None, None),
    )
    return jax.shard_map(
        body, mesh=mesh, in_specs=placed, out_specs=P(("ctx", "head"), None), check_vma=False
    )
```

profile of v0, /device:TPU:160, one launch (start us, length us, event | category | flops | bytes accessed | tf_op | source)
XLA Modules:
  0.0 717.6 jit_solution(11526526723839101949)
XLA Ops:
  0.0 2.8 copy.181
  2.8 4.5 all-to-all-start.1
  8.6 20.2 %all-to-all-done.1 = bf16[96,8,1024]{2,0,1:T(8,128)(2,1)S(1)} async-done(((bf16[96,8,1024]{2,0,1:T(8,128)(2,1)}), bf16[96,8,1024]{2,0,1:T(8,128)(2,1)S(1)}, u32[]{:S(2)}, u32[]{:S(2)}) %all-to-all-start.1) | async-done | bytes 1572896 | tf_op jit(solution)/shard_map/all_to_all | solution.py:83
  28.9 3.6 all-to-all-start.2
  32.4 2.7 copy.182
  35.2 18.8 %all-to-all-done.2 = bf16[96,8,1024]{2,0,1:T(8,128)(2,1)S(1)} async-done(((bf16[96,8,1024]{2,0,1:T(8,128)(2,1)}), bf16[96,8,1024]{2,0,1:T(8,128)(2,1)S(1)}, u32[]{:S(2)}, u32[]{:S(2)}) %all-to-all-start.2) | async-done | bytes 1572896 | tf_op jit(solution)/shard_map/all_to_all | solution.py:84
  53.9 3.6 all-to-all-start
  57.5 3.0 copy.130
  69.6 9.3 %all-to-all-done = bf16[96,8,1024]{2,0,1:T(8,128)(2,1)S(1)} async-done(((bf16[96,8,1024]{2,0,1:T(8,128)(2,1)}), bf16[96,8,1024]{2,0,1:T(8,128)(2,1)S(1)}, u32[]{:S(2)}, u32[]{:S(2)}) %all-to-all-start) | async-done | bytes 1572896 | tf_op jit(solution)/shard_map/all_to_all | solution.py:82
  79.5 5.8 fusion.48
  85.3 424.3 %collective-permute-done.4 = bf16[768,8,128]{2,1,0:T(8,128)(2,1)} collective-permute-done((bf16[768,8,128]{2,1,0:T(8,128)(2,1)}, bf16[768,8,128]{2,1,0:T(8,128)(2,1)}, u32[]{:S(2)}, u32[]{:S(2)}) %collective-permute-start.4) | collective-permute-done | bytes 1572896 | tf_op jit(solution)/shard_map/ppermute | solution.py:18
  511.1 8.9 %fusion.51 = f32[8,768,128]{1,2,0:T(8,128)} fusion(f32[8,768,768]{1,2,0:T(8,128)S(1)} %get-tuple-element.159, f32[8,768]{1,0:T(8,128)S(1)} %get-tuple-element.158, pred[768,768]{0,1:T(8,128)(4,1)S(1)} %copy-done.2, bf16[768,8,128]{2,1,0:T(8,128)(2,1)} %bitcast.54), kind=kOutput, calls=%fused_computation.56 | convolution fusion | flops 1231552512 | bytes 24207360 | tf_op jit(solution)/shard_map/hqk,khd->qhd/dot_general | solution.py:39
  520.1 11.6 %fusion.50 = f32[8,768]{1,0:T(8,128)} fusion(f32[8,768,768]{1,2,0:T(8,128)} %copy-done, f32[8,768]{1,0:T(8,128)S(1)} %get-tuple-element.158, pred[768,768]{0,1:T(8,128)(4,1)S(1)} %copy-done.2), kind=kLoop, calls=%fused_computation.55 | loop fusion | flops 23586816 | bytes 19513344 | tf_op jit(solution)/shard_map/reduce_sum | solution.py:38
  531.7 11.0 %collective-permute-done.5 = bf16[768,8,128]{2,1,0:T(8,128)(2,1)} collective-permute-done((bf16[768,8,128]{2,1,0:T(8,128)(2,1)}, bf16[768,8,128]{2,1,0:T(8,128)(2,1)}, u32[]{:S(2)}, u32[]{:S(2)}) %collective-permute-start.5) | collective-permute-done | bytes 1572896 | tf_op jit(solution)/shard_map/ppermute | solution.py:18
  542.9 48.8 %conditional.5 = (f32[8,768]{1,0:T(8,128)}, f32[8,768]{1,0:T(8,128)}, f32[768,8,128]{0,2,1:T(8,128)}) conditional(s32[]{:T(128)} %convert_element_type.26, () %tuple.33, (s32[3,1,6,6]{3,1,2,0:T(1,128)S(1)}, s32[768,768]{1,0:T(8,128)S(1)}, bf16[768,8,128]{2,1,0:T(8,128)(2,1)}, bf16[768,8,128]{2,1,0:T(8,128)(2,1)}, ...), branch_computations={%region_10.11_spmd, %region_11.14_spmd} | conditional | flops 2477838336 | bytes 81495336 | solution.py:61
  545.0 12.5 %fusion.32 = (f32[8,768]{1,0:T(8,128)}, f32[8,768,768]{1,2,0:T(8,128)}) fusion(pred[768,768]{0,1:T(8,128)(4,1)S(1)} %copy.86, bf16[768,8,128]{2,1,0:T(8,128)(2,1)} %get-tuple-element.141, bf16[768,8,128]{2,1,0:T(8,128)(2,1)} %get-tuple-element.140), kind=kOutput, calls=%fused_computation.36 | convolution fusion | flops 1222109184 | bytes 22634496 | tf_op jit(solution)/shard_map/cond/branch_1_fun/qhd,khd->hqk/dot_general | solution.py:32
  557.5 11.5 %fusion.33 = f32[8,768]{1,0:T(8,128)} fusion(f32[8,768,768]{1,2,0:T(8,128)} %get-tuple-element.153, f32[8,768]{1,0:T(8,128)} %get-tuple-element.163, pred[768,768]{0,1:T(8,128)(4,1)S(1)} %copy.86), kind=kLoop, calls=%fused_computation.37 | loop fusion | flops 23586816 | bytes 19513344 | tf_op jit(solution)/shard_map/cond/branch_1_fun/reduce_sum | solution.py:38
  569.0 11.8 %fusion.38 = f32[768,8,128]{2,0,1:T(8,128)} fusion(f32[8,768,768]{1,2,0:T(8,128)} %get-tuple-element.153, f32[8,768]{1,0:T(8,128)} %get-tuple-element.163, pred[768,768]{0,1:T(8,128)(4,1)S(1)} %copy.86, bf16[768,8,128]{2,1,0:T(8,128)(2,1)} %get-tuple-element.142), kind=kOutput, calls=%fused_computation.42 | convolution fusion | flops 1231552512 | bytes 24207360 | tf_op jit(solution)/shard_map/cond/branch_1_fun/hqk,khd->qhd/dot_general | solution.py:39
  580.8 3.6 copy.121
  591.7 41.8 %conditional.4 = (f32[8,768]{1,0:T(8,128)}, f32[8,768]{1,0:T(8,128)}, f32[768,8,128]{0,2,1:T(8,128)}) conditional(s32[]{:T(128)} %convert_element_type.25, () %tuple.31, (s32[3,1,6,6]{3,1,2,0:T(1,128)S(1)}, s32[768,768]{1,0:T(8,128)S(1)}, bf16[768,8,128]{2,1,0:T(8,128)(2,1)}, bf16[768,8,128]{2,1,0:T(8,128)(2,1)}, ...), branch_computations={%region_6.7_spmd, %region_7.10_spmd} | conditional | flops 2477838336 | bytes 81495336 | solution.py:61
  593.8 12.5 %fusion.16 = (f32[8,768]{1,0:T(8,128)}, f32[8,768,768]{1,2,0:T(8,128)}) fusion(pred[768,768]{0,1:T(8,128)(4,1)S(1)} %copy.84, bf16[768,8,128]{2,1,0:T(8,128)(2,1)} %get-tuple-element.136, bf16[768,8,128]{2,1,0:T(8,128)(2,1)} %get-tuple-element.135), kind=kOutput, calls=%fused_computation.19 | convolution fusion | flops 1222109184 | bytes 22634496 | tf_op jit(solution)/shard_map/cond/branch_1_fun/qhd,khd->hqk/dot_general | solution.py:32
  606.3 11.5 %fusion.17 = f32[8,768]{1,0:T(8,128)} fusion(f32[8,768,768]{1,2,0:T(8,128)} %get-tuple-element.151, f32[8,768]{1,0:T(8,128)} %get-tuple-element.169, pred[768,768]{0,1:T(8,128)(4,1)S(1)} %copy.84), kind=kLoop, calls=%fused_computation.20 | loop fusion | flops 23586816 | bytes 19513344 | tf_op jit(solution)/shard_map/cond/branch_1_fun/reduce_sum | solution.py:38
  617.8 11.9 %fusion.22 = f32[768,8,128]{2,0,1:T(8,128)} fusion(f32[8,768,768]{1,2,0:T(8,128)} %get-tuple-element.151, f32[8,768]{1,0:T(8,128)} %get-tuple-element.169, pred[768,768]{0,1:T(8,128)(4,1)S(1)} %copy.84, bf16[768,8,128]{2,1,0:T(8,128)(2,1)} %get-tuple-element.137), kind=kOutput, calls=%fused_computation.25 | convolution fusion | flops 1231552512 | bytes 24207360 | tf_op jit(solution)/shard_map/cond/branch_1_fun/hqk,khd->qhd/dot_general | solution.py:39
  629.8 3.5 copy.119
  633.6 38.9 %conditional.3 = (f32[8,768]{1,0:T(8,128)S(1)}, f32[8,768]{1,0:T(8,128)S(1)}, f32[768,8,128]{0,2,1:T(8,128)}) conditional(s32[]{:T(128)} %convert_element_type.24, () %tuple.29, (s32[3,1,6,6]{3,1,2,0:T(1,128)S(1)}, s32[768,768]{1,0:T(8,128)S(1)}, bf16[768,8,128]{2,1,0:T(8,128)(2,1)}, bf16[768,8,128]{2,1,0:T(8,128)(2,1)}, ...), branch_computations={%region_2.3_spmd, %region_3.6_spmd} | conditional | flops 2477838336 | bytes 84051320 | solution.py:61
  635.7 12.1 %fusion = (f32[8,768]{1,0:T(8,128)S(1)}, f32[8,768,768]{1,2,0:T(8,128)}) fusion(pred[768,768]{0,1:T(8,128)(4,1)S(1)} %copy.82, bf16[768,8,128]{2,1,0:T(8,128)(2,1)} %get-tuple-element.131, bf16[768,8,128]{2,1,0:T(8,128)(2,1)} %get-tuple-element.130), kind=kOutput, calls=%fused_computation.2 | convolution fusion | flops 1222109184 | bytes 22634496 | tf_op jit(solution)/shard_map/cond/branch_1_fun/qhd,khd->hqk/dot_general | solution.py:32
  647.8 10.9 %fusion.1 = f32[8,768]{1,0:T(8,128)S(1)} fusion(f32[8,768,768]{1,2,0:T(8,128)} %get-tuple-element.149, f32[8,768]{1,0:T(8,128)S(1)} %get-tuple-element.175, pred[768,768]{0,1:T(8,128)(4,1)S(1)} %copy.82), kind=kLoop, calls=%fused_computation.3 | loop fusion | flops 23586816 | bytes 19513344 | tf_op jit(solution)/shard_map/cond/branch_1_fun/reduce_sum | solution.py:38
  658.8 11.0 %fusion.6 = f32[768,8,128]{2,0,1:T(8,128)S(1)} fusion(f32[8,768,768]{1,2,0:T(8,128)} %get-tuple-element.149, f32[8,768]{1,0:T(8,128)S(1)} %get-tuple-element.175, pred[768,768]{0,1:T(8,128)(4,1)} %copy-done.3, bf16[768,8,128]{2,1,0:T(8,128)(2,1)} %get-tuple-element.132), kind=kOutput, calls=%fused_computation.8 | convolution fusion | flops 1231552512 | bytes 24207360 | tf_op jit(solution)/shard_map/cond/branch_1_fun/hqk,khd->qhd/dot_general | solution.py:39
  669.8 2.3 copy.117
  674.1 6.0 fusion.58
  684.5 25.9 %all_to_all.60 = bf16[8,2,49152]{2,1,0:T(2,128)(2,1)} all-to-all(bf16[8,2,49152]{2,1,0:T(2,128)(2,1)S(1)} %reshape.81), channel_id=1, replica_groups=mesh['head'=8,'ctx'=32] {'head'}, dimensions={0} | all-to-all | bytes 3145728 | tf_op jit(solution)/shard_map/all_to_all | solution.py:115
  710.4 4.7 reshape.82
  (62 shorter events, 26.5 us)
Async XLA Ops:
  0.0 7.3 %copy-start.4 = (bf16[96,8192]{1,0:T(8,128)(2,1)S(1)}, bf16[96,8192]{1,0:T(8,128)(2,1)}, u32[]{:S(2)}) copy-start(bf16[96,8192]{1,0:T(8,128)(2,1)} %param.12) | copy-start | bytes 4718596
  2.8 26.0 %all-to-all-start.1 = ((bf16[96,8,1024]{2,0,1:T(8,128)(2,1)}), bf16[96,8,1024]{2,0,1:T(8,128)(2,1)S(1)}, u32[]{:S(2)}, u32[]{:S(2)}) async-start(bf16[96,8,1024]{2,0,1:T(8,128)(2,1)} %bitcast.90), calls=%async_computation.1 | async-start | bytes 3145728 | tf_op jit(solution)/shard_map/all_to_all | solution.py:83
  28.9 25.1 %copy-start.1 = (bf16[96,8,1024]{2,0,1:T(8,128)(2,1)}, bf16[96,8,1024]{2,0,1:T(8,128)(2,1)S(1)}, u32[]{:S(2)}) copy-start(bf16[96,8,1024]{2,0,1:T(8,128)(2,1)S(1)} %all-to-all-done.1) | copy-start | bytes 4718596
  28.9 25.1 %all-to-all-start.2 = ((bf16[96,8,1024]{2,0,1:T(8,128)(2,1)}), bf16[96,8,1024]{2,0,1:T(8,128)(2,1)S(1)}, u32[]{:S(2)}, u32[]{:S(2)}) async-start(bf16[96,8,1024]{2,0,1:T(8,128)(2,1)} %bitcast.98), calls=%async_computation.2 | async-start | bytes 3145728 | tf_op jit(solution)/shard_map/all_to_all | solution.py:84
  53.9 25.1 %all-to-all-start = ((bf16[96,8,1024]{2,0,1:T(8,128)(2,1)}), bf16[96,8,1024]{2,0,1:T(8,128)(2,1)S(1)}, u32[]{:S(2)}, u32[]{:S(2)}) async-start(bf16[96,8,1024]{2,0,1:T(8,128)(2,1)} %bitcast.91), calls=%async_computation | async-start | bytes 3145728 | tf_op jit(solution)/shard_map/all_to_all | solution.py:82
  60.5 449.0 %collective-permute-start.4 = (bf16[768,8,128]{2,1,0:T(8,128)(2,1)}, bf16[768,8,128]{2,1,0:T(8,128)(2,1)}, u32[]{:S(2)}, u32[]{:S(2)}) collective-permute-start(bf16[768,8,128]{2,1,0:T(8,128)(2,1)} %bitcast.49), channel_id=1, source_target_pairs={{0,17},{1,18},{2,19},{3,20},{4,21},{5,22},{6,23},{7,24},{8,25},{9,... | collective-permute-start | bytes 4718600 | tf_op jit(solution)/shard_map/ppermute | solution.py:18
  62.8 528.9 %collective-permute-start.2 = (bf16[768,8,128]{2,1,0:T(8,128)(2,1)}, bf16[768,8,128]{2,1,0:T(8,128)(2,1)}, u32[]{:S(2)}, u32[]{:S(2)}) collective-permute-start(bf16[768,8,128]{2,1,0:T(8,128)(2,1)} %bitcast.49), channel_id=1, source_target_pairs={{0,16},{1,17},{2,18},{3,19},{4,20},{5,21},{6,22},{7,23},{8,24},{9,... | collective-permute-start | bytes 4718600 | tf_op jit(solution)/shard_map/ppermute | solution.py:18
  65.8 477.0 %collective-permute-start.5 = (bf16[768,8,128]{2,1,0:T(8,128)(2,1)}, bf16[768,8,128]{2,1,0:T(8,128)(2,1)}, u32[]{:S(2)}, u32[]{:S(2)}) collective-permute-start(bf16[768,8,128]{2,1,0:T(8,128)(2,1)} %bitcast.54), channel_id=1, source_target_pairs={{0,17},{1,18},{2,19},{3,20},{4,21},{5,22},{6,23},{7,24},{8,25},{9,... | collective-permute-start | bytes 4718600 | tf_op jit(solution)/shard_map/ppermute | solution.py:18
  67.0 524.7 %collective-permute-start.3 = (bf16[768,8,128]{2,1,0:T(8,128)(2,1)}, bf16[768,8,128]{2,1,0:T(8,128)(2,1)}, u32[]{:S(2)}, u32[]{:S(2)}) collective-permute-start(bf16[768,8,128]{2,1,0:T(8,128)(2,1)} %bitcast.54), channel_id=1, source_target_pairs={{0,16},{1,17},{2,18},{3,19},{4,20},{5,21},{6,22},{7,23},{8,24},{9,... | collective-permute-start | bytes 4718600 | tf_op jit(solution)/shard_map/ppermute | solution.py:18
  68.3 565.2 %collective-permute-start = (bf16[768,8,128]{2,1,0:T(8,128)(2,1)}, bf16[768,8,128]{2,1,0:T(8,128)(2,1)}, u32[]{:S(2)}, u32[]{:S(2)}) collective-permute-start(bf16[768,8,128]{2,1,0:T(8,128)(2,1)} %bitcast.49), channel_id=1, source_target_pairs={{0,15},{1,16},{2,17},{3,18},{4,19},{5,20},{6,21},{7,22},{8,23},{9,... | collective-permute-start | bytes 4718600 | tf_op jit(solution)/shard_map/ppermute | solution.py:18
  79.4 5.8 copy-start.5
  79.4 431.7 %copy-start.2 = (pred[768,768]{0,1:T(8,128)(4,1)S(1)}, pred[768,768]{0,1:T(8,128)(4,1)}, u32[]{:S(2)}) copy-start(pred[768,768]{0,1:T(8,128)(4,1)} %iota_compare_fusion) | copy-start | bytes 1769476
  85.2 425.9 %copy-start = (f32[8,768,768]{1,2,0:T(8,128)}, f32[8,768,768]{1,2,0:T(8,128)S(1)}, u32[]{:S(2)}) copy-start(f32[8,768,768]{1,2,0:T(8,128)S(1)} %get-tuple-element.159) | copy-start | bytes 56623108
  85.2 434.8 %copy-start.8 = (f32[8,768]{1,0:T(8,128)}, f32[8,768]{1,0:T(8,128)S(1)}, u32[]{:S(2)}) copy-start(f32[8,768]{1,0:T(8,128)S(1)} %get-tuple-element.158) | copy-start | bytes 73732
  509.6 124.0 %collective-permute-start.1 = (bf16[768,8,128]{2,1,0:T(8,128)(2,1)}, bf16[768,8,128]{2,1,0:T(8,128)(2,1)}, u32[]{:S(2)}, u32[]{:S(2)}) collective-permute-start(bf16[768,8,128]{2,1,0:T(8,128)(2,1)} %bitcast.54), channel_id=1, source_target_pairs={{0,15},{1,16},{2,17},{3,18},{4,19},{5,20},{6,21},{7,22},{8,23},{9,... | collective-permute-start | bytes 4718600 | tf_op jit(solution)/shard_map/ppermute | solution.py:18
  520.1 22.8 %copy-start.11 = (s32[3,1,6,6]{3,1,2,0:T(1,128)S(1)}, s32[3,1,6,6]{3,1,2,0:T(1,128)}, u32[]{:S(2)}) copy-start(s32[3,1,6,6]{3,1,2,0:T(1,128)} %param.13) | copy-start | bytes 1300
  633.6 38.9 %copy-start.9 = (f32[8,768]{1,0:T(8,128)S(1)}, f32[8,768]{1,0:T(8,128)}, u32[]{:S(2)}) copy-start(f32[8,768]{1,0:T(8,128)} %copy-done.8) | copy-start | bytes 73732
  633.6 38.9 %copy-start.10 = (f32[8,768]{1,0:T(8,128)S(1)}, f32[8,768]{1,0:T(8,128)}, u32[]{:S(2)}) copy-start(f32[8,768]{1,0:T(8,128)} %fusion.50) | copy-start | bytes 73732
  635.7 12.1 %copy-start.3 = (pred[768,768]{0,1:T(8,128)(4,1)}, pred[768,768]{0,1:T(8,128)(4,1)S(1)}, u32[]{:S(2)}) copy-start(pred[768,768]{0,1:T(8,128)(4,1)S(1)} %copy.82) | copy-start | bytes 1769476 | tf_op jit(solution)/shard_map/cond
  647.8 10.9 %copy-start.6 = (f32[8,768]{1,0:T(8,128)}, f32[8,768]{1,0:T(8,128)S(1)}, u32[]{:S(2)}) copy-start(f32[8,768]{1,0:T(8,128)S(1)} %get-tuple-element.175) | copy-start | bytes 73732 | tf_op jit(solution)/shard_map/cond
  669.8 2.4 copy-start.7
where the time goes:
time: 723 us; the launch traced here: 718 us
  waiting for transfers between devices  484 us (67%)
  matrix products  86.6 us (12%)
  other arithmetic  58.3 us (8%)
  local copies, waits for them, and re-layouts  34.6 us (5%)
  blocking collectives  25.9 us (4%)
  starting transfers between devices  19.6 us (3%)
  loops' own time  8.04 us (1%)
    ppermute x6, waiting for transfers between devices, from_behind(): lax.ppermute(value, axis, [(source, source + steps) for source in range(l...  435 us
    reduce_sum x4, other arithmetic, partial_block(): totals = jnp.sum(expo, axis=2)  45.6 us
    dot_general x4, matrix products, partial_block(): jnp.einsum('hqk,khd->qhd', expo.astype(jnp.bfloat16), head_values, prefer...  43.7 us
    dot_general x4, matrix products, partial_block(): jnp.einsum('qhd,khd->hqk', head_queries, head_keys, preferred_element_typ...  42.9 us
    all_to_all x1, blocking collectives, body(): lax.all_to_all(combined.reshape(C, 1, local_heads * HD), 'head', split_ax...  25.9 us
    all_to_all x1, waiting for transfers between devices, body(): lax.all_to_all(regroup(keys, groups), 'head', split_axis=1, concat_axis=0...  20.2 us
    all_to_all x1, waiting for transfers between devices, body(): lax.all_to_all(regroup(values, groups), 'head', split_axis=1, concat_axis...  18.8 us
  transfers between devices with their start and end apart: 9, of which 5 were waited for; matrix products, arithmetic and copies ran while one was open for 17% of the time, Pallas kernels for 0%

commit v1 on v0

v1 whole, which is shorter than its diff:
```python
import functools
import math

import jax
import jax.numpy as jnp
from jax import lax
from jax.experimental import pallas as pl
from jax.experimental.pallas import tpu as pltpu
from jax.sharding import PartitionSpec as P


H = 64
HD = 128
BLOCK = 128
C = 768
QB = C // BLOCK
CHUNKS = 4
ROWS = 256
STEPS = C // ROWS
TAIL = 24
NEG = -1e30
FACTOR = HD**-0.5 * math.log2(math.e)


def eye():
    return lax.broadcasted_iota(jnp.int32, (BLOCK, BLOCK), 0) == lax.broadcasted_iota(
        jnp.int32, (BLOCK, BLOCK), 1
    )


def dot_t(a, b):
    return lax.dot_general(a, b, (((1,), (1,)), ((), ())), preferred_element_type=jnp.float32)


def far_kernel(
    active, q_ref, ka_ref, va_ref, kb_ref, vb_ref, kc_ref, vc_ref, bias_ref, o_ref, vx_ref, lse_ref
):
    step = pl.program_id(1)

    @pl.when(active[0] > 0)
    def _():
        @pl.when(step == 0)
        def _():
            for i, v_ref in enumerate((va_ref, vb_ref, vc_ref)):
                vx_ref[i, :, :HD] = v_ref[...]
                vx_ref[i, :, HD:] = jnp.ones((C, HD), jnp.bfloat16)
            lse_ref[...] = jnp.zeros_like(lse_ref)

        q = q_ref[...]
        scores = []
        for i, k_ref in enumerate((ka_ref, kb_ref, kc_ref)):
            raw = dot_t(q, k_ref[...]) * FACTOR
            parts = [
                raw[r * BLOCK : (r + 1) * BLOCK]
                + bias_ref[pl.ds(step * (ROWS // BLOCK) + r, 1), i * C : (i + 1) * C]
                for r in range(ROWS // BLOCK)
            ]
            scores.append(jnp.concatenate(parts, 0))
        top = functools.reduce(
            jnp.maximum, [jnp.max(s, axis=1, keepdims=True) for s in scores]
        )
        total = jnp.zeros((ROWS, 2 * HD), jnp.float32)
        for i, s in enumerate(scores):
            p = jnp.exp2(s - top).astype(jnp.bfloat16)
            total = total + jnp.dot(p, vx_ref[i], preferred_element_type=jnp.float32)
        sums = total[:, HD:]
        start = pl.multiple_of(step * ROWS, ROWS)
        o_ref[pl.ds(start, ROWS), :] = (total[:, :HD] / sums).astype(jnp.bfloat16)
        lse = top + jnp.log2(sums)
        for r in range(ROWS // BLOCK):
            line = jnp.sum(
                jnp.where(eye(), lse[r * BLOCK : (r + 1) * BLOCK], 0.0), axis=0, keepdims=True
            )
            lse_ref[pl.ds(step * (ROWS // BLOCK) + r, 1), :] = line

        @pl.when(step == STEPS - 1)
        def _():
            rest = lse_ref[...]
            terms = []
            for _ in range(3):
                term = rest.astype(jnp.bfloat16).astype(jnp.float32)
                terms.append(term)
                rest = rest - term
            o_ref[C:, :] = jnp.concatenate(terms, 0).astype(jnp.bfloat16)


def pack_kernel(groups, cols, n, *refs):
    *sources, packed, sem = refs
    width = sources[0].shape[1] // groups
    copies = []
    for i, source in enumerate(sources):
        for g in range(groups):
            copies.append(
                pltpu.make_async_copy(
                    source.at[:, pl.ds(g * width + n * cols, cols)],
                    packed.at[g, :, pl.ds(i * cols, cols)],
                    sem.at[i, g],
                )
            )
    for copy in copies:
        copy.start()
    for copy in copies:
        copy.wait()


def pack(sources, groups, cols, n):
    rows = sources[0].shape[0]
    return pl.pallas_call(
        functools.partial(pack_kernel, groups, cols, n),
        out_shape=jax.ShapeDtypeStruct((groups, rows, len(sources) * cols), jnp.bfloat16),
        in_specs=[pl.BlockSpec(memory_space=pl.ANY)] * len(sources),
        out_specs=pl.BlockSpec(memory_space=pl.ANY),
        scratch_shapes=[pltpu.SemaphoreType.DMA((len(sources), groups))],
        name="pack",
    )(*sources)


def unpack_kernel(groups, cols, n, *refs):
    piece, whole, sem = refs[0], refs[-2], refs[-1]
    width = whole.shape[1] // groups
    copies = [
        pltpu.make_async_copy(
            piece.at[g], whole.at[:, pl.ds(g * width + n * cols, cols)], sem.at[g]
        )
        for g in range(groups)
    ]
    for copy in copies:
        copy.start()
    for copy in copies:
        copy.wait()


def unpack(piece, whole, width, n):
    groups, rows, cols = piece.shape
    operands = (piece,) if whole is None else (piece, whole)
    return pl.pallas_call(
        functools.partial(unpack_kernel, groups, cols, n),
        out_shape=jax.ShapeDtypeStruct((rows, width), jnp.bfloat16),
        in_specs=[pl.BlockSpec(memory_space=pl.ANY)] * len(operands),
        out_specs=pl.BlockSpec(memory_space=pl.ANY),
        scratch_shapes=[pltpu.SemaphoreType.DMA((groups,))],
        input_output_aliases={} if whole is None else {1: 0},
        name="unpack",
    )(*operands)


def far_attention(active, far_q, own, before, after, bias, heads):
    def kv(part):
        return pl.BlockSpec((C, HD), lambda h, s, *_: (0, part * heads + h))

    return pl.pallas_call(
        far_kernel,
        out_shape=jax.ShapeDtypeStruct((C + TAIL, heads * HD), jnp.bfloat16),
        grid_spec=pltpu.PrefetchScalarGridSpec(
            num_scalar_prefetch=1,
            grid=(heads, STEPS),
            in_specs=[
                pl.BlockSpec((ROWS, HD), lambda h, s, *_: (s, h)),
                kv(0), kv(1), kv(0), kv(1), kv(0), kv(1),
                pl.BlockSpec((8, 3 * C), lambda h, s, *_: (0, 0)),
            ],
            out_specs=pl.BlockSpec((C + TAIL, HD), lambda h, s, *_: (0, h)),
            scratch_shapes=[
                pltpu.VMEM((3, C, 2 * HD), jnp.bfloat16),
                pltpu.VMEM((8, BLOCK), jnp.float32),
            ],
        ),
        name="far_attention",
    )(active, far_q, after, after, own, own, before, before, bias)


def near_kernel(receives, q_ref, k_ref, v_ref, far_ref, o_ref, vx_ref):
    vx_ref[:, :HD] = v_ref[...]
    vx_ref[:, HD:] = jnp.ones((C, HD), jnp.bfloat16)
    tail = far_ref[C:, :].astype(jnp.float32)
    lse_all = tail[0:8] + (tail[8:16] + tail[16:24])
    lse_all = jnp.where(receives[0] > 0, lse_all, NEG)
    for step in range(STEPS):
        lo, hi = step * ROWS, (step + 1) * ROWS
        s = dot_t(q_ref[lo:hi, :], k_ref[:hi, :]) * FACTOR
        rows = lo + lax.broadcasted_iota(jnp.int32, (ROWS, hi), 0)
        cols = lax.broadcasted_iota(jnp.int32, (ROWS, hi), 1)
        s = jnp.where(rows >= cols, s, NEG)
        top = jnp.max(s, axis=1, keepdims=True)
        p = jnp.exp2(s - top).astype(jnp.bfloat16)
        total = jnp.dot(p, vx_ref[:hi, :], preferred_element_type=jnp.float32)
        columns = []
        for r in range(ROWS // BLOCK):
            line = lse_all[step * (ROWS // BLOCK) + r][None, :]
            columns.append(jnp.sum(jnp.where(eye(), line, 0.0), axis=1, keepdims=True))
        far_lse = jnp.concatenate(columns, 0)
        peak = jnp.maximum(top, far_lse)
        near_w = jnp.exp2(top - peak)
        far_w = jnp.exp2(far_lse - peak)
        far_o = far_ref[lo:hi, :].astype(jnp.float32)
        upper = total[:, :HD] * near_w + far_o * far_w
        lower = total[:, HD:] * near_w + far_w
        o_ref[lo:hi, :] = (upper / lower).astype(jnp.bfloat16)


def near_attention(receives, q, kv, far, heads):
    return pl.pallas_call(
        near_kernel,
        out_shape=jax.ShapeDtypeStruct((C, heads * HD), jnp.bfloat16),
        grid_spec=pltpu.PrefetchScalarGridSpec(
            num_scalar_prefetch=1,
            grid=(heads,),
            in_specs=[
                pl.BlockSpec((C, HD), lambda h, *_: (0, h)),
                pl.BlockSpec((C, HD), lambda h, *_: (0, h)),
                pl.BlockSpec((C, HD), lambda h, *_: (0, heads + h)),
                pl.BlockSpec((C + TAIL, HD), lambda h, *_: (0, h)),
            ],
            out_specs=pl.BlockSpec((C, HD), lambda h, *_: (0, h)),
            scratch_shapes=[pltpu.VMEM((C, 2 * HD), jnp.bfloat16)],
        ),
        name="near_attention",
    )(receives, q, kv, kv, far)


def layer(queries, keys, values, pattern):
    groups = lax.axis_size("head")
    spans = lax.axis_size("ctx")
    position = lax.axis_index("ctx")
    far = spans // 2
    tok_rows, width = queries.shape
    heads = H // groups // CHUNKS
    cols = heads * HD
    there = [(c, (c - far) % spans) for c in range(far - 1, spans)]
    back = [(b, a) for a, b in there]
    helpers = sorted(b for _, b in there)
    from_before = [(b - 1, b) for b in helpers if b - 1 in range(far)]
    from_after = [((b + 1) % spans, b) for b in helpers]
    receives = (position >= far - 1).astype(jnp.int32)[None]
    active = ((position < far) | (position == spans - 1)).astype(jnp.int32)[None]

    distances = jnp.array([far - 1, far, far + 1], jnp.int32)
    flags = jnp.where(position >= distances[:, None, None], pattern[:, 0], 0)
    flags = lax.ppermute(flags, "ctx", there)
    lines = jnp.where(flags.transpose(1, 0, 2).reshape(QB, 3 * QB) == 1, 0.0, NEG)
    bias = jnp.repeat(jnp.pad(lines, ((0, 2), (0, 0))), BLOCK, axis=1)

    whole = None
    for n in range(CHUNKS):
        packed = pack((queries, keys, values), groups, cols, n)
        packed = lax.all_to_all(packed, "head", split_axis=0, concat_axis=0, tiled=True)
        packed = packed.reshape(C, 3 * cols)
        q, kv = packed[:, :cols], packed[:, cols:]
        far_q = lax.ppermute(q, "ctx", there)
        before = lax.ppermute(kv, "ctx", from_before)
        after = lax.ppermute(kv, "ctx", from_after)
        far_o = far_attention(active, far_q, kv, before, after, bias, heads)
        far_o = lax.ppermute(far_o, "ctx", back)
        out = near_attention(receives, q, kv, far_o, heads)
        out = lax.all_to_all(
            out.reshape(groups, tok_rows, cols), "head", split_axis=0, concat_axis=0, tiled=True
        )
        whole = unpack(out, whole, width, n)
    return whole


def solution(mesh):
    placed = (
        P(("ctx", "head"), None),
        P(("ctx", "head"), None),
        P(("ctx", "head"), None),
        P(None, "ctx", None, None),
    )
    return jax.shard_map(
        layer, mesh=mesh, in_specs=placed, out_specs=P(("ctx", "head"), None), check_vma=False
    )
```

time: 723 us -> 401 us (0.55)
  the two profiles are of different devices: /device:TPU:160 before, /device:TPU:111 now
where the time goes in v1:
time: 401 us; the launch traced here: 400 us
  Pallas kernels  267 us (67%)
  starting transfers between devices  105 us (26%)
  local copies, waits for them, and re-layouts  13.8 us (3%)
  waiting for transfers between devices  12.5 us (3%)
    pallas_call x4, Pallas kernels, pack(): pl.pallas_call(functools.partial(pack_kernel, groups, cols, n), out_shape...  148 us
    pallas_call x4, Pallas kernels, unpack(): pl.pallas_call(functools.partial(unpack_kernel, groups, cols, n), out_sha...  52.3 us
    pallas_call x4, Pallas kernels, far_attention(): pl.pallas_call(far_kernel, out_shape=jax.ShapeDtypeStruct((C + TAIL, head...  48.5 us
    all_to_all x4, starting transfers between devices, layer(): lax.all_to_all(out.reshape(groups, tok_rows, cols), 'head', split_axis=0,...  23.2 us
    ppermute x4, starting transfers between devices, layer(): far_o = lax.ppermute(far_o, 'ctx', back)  22.1 us
    all_to_all x4, starting transfers between devices, layer(): lax.all_to_all(packed, 'head', split_axis=0, concat_axis=0, tiled=True)  20.5 us
    ppermute x4, starting transfers between devices, layer(): far_q = lax.ppermute(q, 'ctx', there)  18.6 us
    pallas_call x4, Pallas kernels, near_attention(): pl.pallas_call(near_kernel, out_shape=jax.ShapeDtypeStruct((C, heads * HD...  18.4 us
  transfers between devices with their start and end apart: 25, of which 3 were waited for; matrix products, arithmetic and copies ran while one was open for 2% of the time, Pallas kernels for 54%

profile of v1, /device:TPU:111, one launch (start us, length us, event | category | flops | bytes accessed | tf_op | source)
XLA Modules:
  0.0 399.6 jit_solution(12494510775901287927)
XLA Ops:
  0.0 37.0 %pack.5 = bf16[8,96,768]{2,1,0:T(8,128)(2,1)} custom-call(bf16[96,8192]{1,0:T(8,128)(2,1)} %refs_0_.7, bf16[96,8192]{1,0:T(8,128)(2,1)} %refs_1_.7, bf16[96,8192]{1,0:T(8,128)(2,1)} %refs_2_.7), custom_call_target="tpu_custom_call" | custom-call | tf_op jit(solution)/shard_map/pack/pallas_call | solution.py:108
  37.1 5.2 %all-to-all-start.2 = ((bf16[8,96,768]{2,1,0:T(8,128)(2,1)}), bf16[8,96,768]{2,1,0:T(8,128)(2,1)S(1)}, u32[]{:S(2)}, u32[]{:S(2)}) async-start(bf16[8,96,768]{2,1,0:T(8,128)(2,1)} %pack.5), calls=%async_computation.2 | async-start | bytes 2359296 | tf_op jit(solution)/shard_map/all_to_all | solution.py:246
  42.3 37.0 %pack.6 = bf16[8,96,768]{2,1,0:T(8,128)(2,1)} custom-call(bf16[96,8192]{1,0:T(8,128)(2,1)} %refs_0_.7, bf16[96,8192]{1,0:T(8,128)(2,1)} %refs_1_.7, bf16[96,8192]{1,0:T(8,128)(2,1)} %refs_2_.7), custom_call_target="tpu_custom_call" | custom-call | tf_op jit(solution)/shard_map/pack/pallas_call | solution.py:108
  80.3 4.8 %all-to-all-start.4 = ((bf16[8,96,768]{2,1,0:T(8,128)(2,1)}), bf16[8,96,768]{2,1,0:T(8,128)(2,1)S(1)}, u32[]{:S(2)}, u32[]{:S(2)}) async-start(bf16[8,96,768]{2,1,0:T(8,128)(2,1)} %pack.6), calls=%async_computation.4 | async-start | bytes 2359296 | tf_op jit(solution)/shard_map/all_to_all | solution.py:246
  85.2 37.0 %pack.7 = bf16[8,96,768]{2,1,0:T(8,128)(2,1)} custom-call(bf16[96,8192]{1,0:T(8,128)(2,1)} %refs_0_.7, bf16[96,8192]{1,0:T(8,128)(2,1)} %refs_1_.7, bf16[96,8192]{1,0:T(8,128)(2,1)} %refs_2_.7), custom_call_target="tpu_custom_call" | custom-call | tf_op jit(solution)/shard_map/pack/pallas_call | solution.py:108
  122.2 4.8 %all-to-all-start.6 = ((bf16[8,96,768]{2,1,0:T(8,128)(2,1)}), bf16[8,96,768]{2,1,0:T(8,128)(2,1)S(1)}, u32[]{:S(2)}, u32[]{:S(2)}) async-start(bf16[8,96,768]{2,1,0:T(8,128)(2,1)} %pack.7), calls=%async_computation.6 | async-start | bytes 2359296 | tf_op jit(solution)/shard_map/all_to_all | solution.py:246
  134.0 5.2 %collective-permute-start.5 = (bf16[768,256]{1,0:T(8,128)(2,1)}, bf16[768,256]{1,0:T(8,128)(2,1)}, u32[]{:S(2)}, u32[]{:S(2)}) collective-permute-start(bf16[768,256]{1,0:T(8,128)(2,1)} %slice.34.q_ref), channel_id=1, source_target_pairs={{15,31},{16,0},{17,1},{18,2},{19,3},{20,4},{21,5},{22,6},{23,7},{2... | collective-permute-start | bytes 1179656 | tf_op jit(solution)/shard_map/ppermute | solution.py:249
  140.0 4.0 collective-permute-start.9
  144.1 5.2 %collective-permute-start.3 = (s32[3,6,6]{2,1,0:T(8,128)S(1)}, s32[3,6,6]{2,1,0:T(8,128)S(1)}, u32[]{:S(2)}, u32[]{:S(2)}) collective-permute-start(s32[3,6,6]{2,1,0:T(8,128)S(1)} %bitcast_select_fusion), channel_id=1, source_target_pairs={{15,31},{16,0},{17,1},{18,2},{19,3},{20,4},{21,5},{22,6},{23,7},{2... | collective-permute-start | bytes 1304 | tf_op jit(solution)/shard_map/ppermute | solution.py:239
  149.2 37.1 %pack.4 = bf16[8,96,768]{2,1,0:T(8,128)(2,1)} custom-call(bf16[96,8192]{1,0:T(8,128)(2,1)} %refs_0_.7, bf16[96,8192]{1,0:T(8,128)(2,1)} %refs_1_.7, bf16[96,8192]{1,0:T(8,128)(2,1)} %refs_2_.7), custom_call_target="tpu_custom_call" | custom-call | tf_op jit(solution)/shard_map/pack/pallas_call | solution.py:108
  187.4 5.6 %all-to-all-start = ((bf16[8,96,768]{2,1,0:T(8,128)(2,1)}), bf16[8,96,768]{2,1,0:T(8,128)(2,1)S(1)}, u32[]{:S(2)}, u32[]{:S(2)}) async-start(bf16[8,96,768]{2,1,0:T(8,128)(2,1)} %pack.4), calls=%async_computation | async-start | bytes 2359296 | tf_op jit(solution)/shard_map/all_to_all | solution.py:246
  198.8 4.0 collective-permute-start.14
  206.7 12.1 %far_attention.5 = bf16[792,256]{1,0:T(8,128)(2,1)} custom-call(s32[1]{0:T(128)} %bitcast.2.active, bf16[768,256]{1,0:T(8,128)(2,1)} %collective-permute-done.5.q_ref, bf16[768,512]{1,0:T(8,128)(2,1)} %collective-permute-done.6.ka_ref.va_ref, bf16[768,512]{1,0:T(8,128)(2,1)} %collective-permute-done.6.ka_ref.va_ref, bf16[768,512]{1,0:T(8,128)(2,1)} %copy-done.1, ...), custom_call_target="tpu_custom_call" | custom-call | tf_op jit(solution)/shard_map/far_attention/pallas_call | solution.py:151
  219.8 6.3 %collective-permute-start.8 = (bf16[792,256]{1,0:T(8,128)(2,1)}, bf16[792,256]{1,0:T(8,128)(2,1)}, u32[]{:S(2)}, u32[]{:S(2)}) collective-permute-start(bf16[792,256]{1,0:T(8,128)(2,1)} %far_attention.5), channel_id=1, source_target_pairs={{31,15},{0,16},{1,17},{2,18},{3,19},{4,20},{5,21},{6,22},{7,23},{8... | collective-permute-start | bytes 1216520 | tf_op jit(solution)/shard_map/ppermute | solution.py:253
  226.2 10.2 %collective-permute-done.10.ka_ref.va_ref = bf16[768,512]{1,0:T(8,128)(2,1)} collective-permute-done((bf16[768,512]{1,0:T(8,128)(2,1)S(1)}, bf16[768,512]{1,0:T(8,128)(2,1)}, u32[]{:S(2)}, u32[]{:S(2)}) %collective-permute-start.10) | collective-permute-done | bytes 786464 | tf_op jit(solution)/shard_map/ppermute | solution.py:251
  239.6 12.2 %far_attention.6 = bf16[792,256]{1,0:T(8,128)(2,1)} custom-call(s32[1]{0:T(128)} %bitcast.2.active, bf16[768,256]{1,0:T(8,128)(2,1)} %collective-permute-done.9.q_ref, bf16[768,512]{1,0:T(8,128)(2,1)} %collective-permute-done.10.ka_ref.va_ref, bf16[768,512]{1,0:T(8,128)(2,1)} %collective-permute-done.10.ka_ref.va_ref, bf16[768,512]{1,0:T(8,128)(2,1)} %copy-done.2, ...), custom_call_target="tpu_custom_call" | custom-call | tf_op jit(solution)/shard_map/far_attention/pallas_call | solution.py:151
  253.7 4.6 %near_attention.5 = bf16[768,256]{1,0:T(8,128)(2,1)} custom-call(s32[1]{0:T(128)} %bitcast.receives, bf16[768,256]{1,0:T(8,128)(2,1)} %slice.34.q_ref, bf16[768,512]{1,0:T(8,128)(2,1)} %copy-done.1, bf16[768,512]{1,0:T(8,128)(2,1)} %copy-done.1, bf16[792,256]{1,0:T(8,128)(2,1)} %collective-permute-done.8.far_ref), custom_call_target="tpu_custom_call" | custom-call | tf_op jit(solution)/shard_map/near_attention/pallas_call | solution.py:202
  258.3 6.5 %all-to-all-start.3 = ((bf16[8,96,256]{2,1,0:T(8,128)(2,1)}), bf16[8,96,256]{2,1,0:T(8,128)(2,1)}, u32[]{:S(2)}, u32[]{:S(2)}) async-start(bf16[8,96,256]{2,1,0:T(8,128)(2,1)} %bitcast.27), calls=%async_computation.3 | async-start | bytes 786432 | tf_op jit(solution)/shard_map/all_to_all | solution.py:255
  265.6 7.5 %collective-permute-start = (bf16[768,256]{1,0:T(8,128)(2,1)}, bf16[768,256]{1,0:T(8,128)(2,1)S(1)}, u32[]{:S(2)}, u32[]{:S(2)}) collective-permute-start(bf16[768,256]{1,0:T(8,128)(2,1)} %slice.32.q_ref), channel_id=1, source_target_pairs={{15,31},{16,0},{17,1},{18,2},{19,3},{20,4},{21,5},{22,6},{23,7},{2... | collective-permute-start | bytes 1179656 | tf_op jit(solution)/shard_map/ppermute | solution.py:249
  273.1 12.1 %far_attention.7 = bf16[792,256]{1,0:T(8,128)(2,1)} custom-call(s32[1]{0:T(128)} %bitcast.2.active, bf16[768,256]{1,0:T(8,128)(2,1)} %copy-done.14, bf16[768,512]{1,0:T(8,128)(2,1)} %collective-permute-done.14.ka_ref.va_ref, bf16[768,512]{1,0:T(8,128)(2,1)} %collective-permute-done.14.ka_ref.va_ref, bf16[768,512]{1,0:T(8,128)(2,1)} %copy-done, ...), custom_call_target="tpu_custom_call" | custom-call | tf_op jit(solution)/shard_map/far_attention/pallas_call | solution.py:151
  287.2 4.6 %near_attention.6 = bf16[768,256]{1,0:T(8,128)(2,1)} custom-call(s32[1]{0:T(128)} %bitcast.receives, bf16[768,256]{1,0:T(8,128)(2,1)} %slice.36.q_ref, bf16[768,512]{1,0:T(8,128)(2,1)} %copy-done.2, bf16[768,512]{1,0:T(8,128)(2,1)} %copy-done.2, bf16[792,256]{1,0:T(8,128)(2,1)} %collective-permute-done.12.far_ref), custom_call_target="tpu_custom_call" | custom-call | tf_op jit(solution)/shard_map/near_attention/pallas_call | solution.py:202
  291.8 5.1 %all-to-all-start.5 = ((bf16[8,96,256]{2,1,0:T(8,128)(2,1)}), bf16[8,96,256]{2,1,0:T(8,128)(2,1)S(1)}, u32[]{:S(2)}, u32[]{:S(2)}) async-start(bf16[8,96,256]{2,1,0:T(8,128)(2,1)} %bitcast.26), calls=%async_computation.5 | async-start | bytes 786432 | tf_op jit(solution)/shard_map/all_to_all | solution.py:255
  298.6 12.1 %far_attention.4 = bf16[792,256]{1,0:T(8,128)(2,1)} custom-call(s32[1]{0:T(128)} %bitcast.2.active, bf16[768,256]{1,0:T(8,128)(2,1)} %copy-done.15, bf16[768,512]{1,0:T(8,128)(2,1)} %collective-permute-done.1.ka_ref.va_ref, bf16[768,512]{1,0:T(8,128)(2,1)} %collective-permute-done.1.ka_ref.va_ref, bf16[768,512]{1,0:T(8,128)(2,1)} %copy-done.3, ...), custom_call_target="tpu_custom_call" | custom-call | tf_op jit(solution)/shard_map/far_attention/pallas_call | solution.py:151
  310.8 12.0 %collective-permute-start.4 = (bf16[792,256]{1,0:T(8,128)(2,1)}, bf16[792,256]{1,0:T(8,128)(2,1)S(1)}, u32[]{:S(2)}, u32[]{:S(2)}) collective-permute-start(bf16[792,256]{1,0:T(8,128)(2,1)} %far_attention.4), channel_id=1, source_target_pairs={{31,15},{0,16},{1,17},{2,18},{3,19},{4,20},{5,21},{6,22},{7,23},{8... | collective-permute-start | bytes 1216520 | tf_op jit(solution)/shard_map/ppermute | solution.py:253
  323.5 4.6 %near_attention.7 = bf16[768,256]{1,0:T(8,128)(2,1)} custom-call(s32[1]{0:T(128)} %bitcast.receives, bf16[768,256]{1,0:T(8,128)(2,1)} %slice.38.q_ref, bf16[768,512]{1,0:T(8,128)(2,1)} %copy-done, bf16[768,512]{1,0:T(8,128)(2,1)} %copy-done, bf16[792,256]{1,0:T(8,128)(2,1)} %copy-done.12), custom_call_target="tpu_custom_call" | custom-call | tf_op jit(solution)/shard_map/near_attention/pallas_call | solution.py:202
  328.1 5.9 %all-to-all-start.7 = ((bf16[8,96,256]{2,1,0:T(8,128)(2,1)}), bf16[8,96,256]{2,1,0:T(8,128)(2,1)S(1)}, u32[]{:S(2)}, u32[]{:S(2)}) async-start(bf16[8,96,256]{2,1,0:T(8,128)(2,1)} %bitcast.28), calls=%async_computation.7 | async-start | bytes 786432 | tf_op jit(solution)/shard_map/all_to_all | solution.py:255
  334.9 4.6 %near_attention.4 = bf16[768,256]{1,0:T(8,128)(2,1)} custom-call(s32[1]{0:T(128)} %bitcast.receives, bf16[768,256]{1,0:T(8,128)(2,1)} %slice.32.q_ref, bf16[768,512]{1,0:T(8,128)(2,1)} %copy-done.3, bf16[768,512]{1,0:T(8,128)(2,1)} %copy-done.3, bf16[792,256]{1,0:T(8,128)(2,1)} %copy-done.13), custom_call_target="tpu_custom_call" | custom-call | tf_op jit(solution)/shard_map/near_attention/pallas_call | solution.py:202
  340.7 5.7 %all-to-all-start.1 = ((bf16[8,96,256]{2,1,0:T(8,128)(2,1)}), bf16[8,96,256]{2,1,0:T(8,128)(2,1)S(1)}, u32[]{:S(2)}, u32[]{:S(2)}) async-start(bf16[8,96,256]{2,1,0:T(8,128)(2,1)} %bitcast.29), calls=%async_computation.1 | async-start | bytes 786432 | tf_op jit(solution)/shard_map/all_to_all | solution.py:255
  346.4 13.1 %unpack.4.refs_1_ = bf16[96,8192]{1,0:T(8,128)(2,1)} custom-call(bf16[8,96,256]{2,1,0:T(8,128)(2,1)} %copy-done.11), custom_call_target="tpu_custom_call" | custom-call | tf_op jit(solution)/shard_map/unpack/pallas_call | solution.py:136
  359.5 13.1 %unpack.5.refs_1_ = bf16[96,8192]{1,0:T(8,128)(2,1)} custom-call(bf16[8,96,256]{2,1,0:T(8,128)(2,1)} %copy-done.9, bf16[96,8192]{1,0:T(8,128)(2,1)} %unpack.4.refs_1_), custom_call_target="tpu_custom_call", output_to_operand_aliasing={{}: (1, {})} | custom-call | tf_op jit(solution)/shard_map/unpack/pallas_call | solution.py:136
  372.6 13.1 %unpack.6.refs_1_ = bf16[96,8192]{1,0:T(8,128)(2,1)} custom-call(bf16[8,96,256]{2,1,0:T(8,128)(2,1)} %all-to-all-done.3.refs_0_, bf16[96,8192]{1,0:T(8,128)(2,1)} %unpack.5.refs_1_), custom_call_target="tpu_custom_call", output_to_operand_aliasing={{}: (1, {})} | custom-call | tf_op jit(solution)/shard_map/unpack/pallas_call | solution.py:136
  386.4 13.1 %unpack.7 = bf16[96,8192]{1,0:T(8,128)(2,1)} custom-call(bf16[8,96,256]{2,1,0:T(8,128)(2,1)} %copy-done.10, bf16[96,8192]{1,0:T(8,128)(2,1)} %unpack.6.refs_1_), custom_call_target="tpu_custom_call", output_to_operand_aliasing={{}: (1, {})} | custom-call | tf_op jit(solution)/shard_map/unpack/pallas_call | solution.py:136
  (85 shorter events, 33.5 us)
Async XLA Ops:
  37.1 42.3 %all-to-all-start.2 = ((bf16[8,96,768]{2,1,0:T(8,128)(2,1)}), bf16[8,96,768]{2,1,0:T(8,128)(2,1)S(1)}, u32[]{:S(2)}, u32[]{:S(2)}) async-start(bf16[8,96,768]{2,1,0:T(8,128)(2,1)} %pack.5), calls=%async_computation.2 | async-start | bytes 2359296 | tf_op jit(solution)/shard_map/all_to_all | solution.py:246
  80.3 41.9 %all-to-all-start.4 = ((bf16[8,96,768]{2,1,0:T(8,128)(2,1)}), bf16[8,96,768]{2,1,0:T(8,128)(2,1)S(1)}, u32[]{:S(2)}, u32[]{:S(2)}) async-start(bf16[8,96,768]{2,1,0:T(8,128)(2,1)} %pack.6), calls=%async_computation.4 | async-start | bytes 2359296 | tf_op jit(solution)/shard_map/all_to_all | solution.py:246
  122.2 16.9 %copy-start.4 = (bf16[8,96,768]{2,1,0:T(8,128)(2,1)}, bf16[8,96,768]{2,1,0:T(8,128)(2,1)S(1)}, u32[]{:S(2)}) copy-start(bf16[8,96,768]{2,1,0:T(8,128)(2,1)S(1)} %all-to-all-done.4) | copy-start | bytes 3538948
  122.2 64.1 %all-to-all-start.6 = ((bf16[8,96,768]{2,1,0:T(8,128)(2,1)}), bf16[8,96,768]{2,1,0:T(8,128)(2,1)S(1)}, u32[]{:S(2)}, u32[]{:S(2)}) async-start(bf16[8,96,768]{2,1,0:T(8,128)(2,1)} %pack.7), calls=%async_computation.6 | async-start | bytes 2359296 | tf_op jit(solution)/shard_map/all_to_all | solution.py:246
  128.2 58.1 %copy-start.1 = (bf16[768,512]{1,0:T(8,128)(2,1)}, bf16[768,512]{1,0:T(8,128)(2,1)S(1)}, u32[]{:S(2)}) copy-start(bf16[768,512]{1,0:T(8,128)(2,1)S(1)} %slice.35.kb_ref.vb_ref.k_ref.v_ref) | copy-start | bytes 2359300
  128.3 15.7 %copy-start.16 = (s32[3,1,6,6]{3,1,2,0:T(1,128)S(1)}, s32[3,1,6,6]{3,1,2,0:T(1,128)}, u32[]{:S(2)}) copy-start(s32[3,1,6,6]{3,1,2,0:T(1,128)} %param.8) | copy-start | bytes 1300
  128.3 74.5 %collective-permute-start.6 = (bf16[768,512]{1,0:T(8,128)(2,1)S(1)}, bf16[768,512]{1,0:T(8,128)(2,1)}, u32[]{:S(2)}, u32[]{:S(2)}) collective-permute-start(bf16[768,512]{1,0:T(8,128)(2,1)S(1)} %slice.35.kb_ref.vb_ref.k_ref.v_ref), channel_id=1, source_target_pairs={{1,0},{2,1},{3,2},{4,3},{5,4},{6,5},{7,6},{8,7},{9,8},{10,9},{11,1... | collective-permute-start | bytes 2359304 | tf_op jit(solution)/shard_map/ppermute | solution.py:251
  130.9 73.2 %collective-permute-start.7 = (bf16[768,512]{1,0:T(8,128)(2,1)S(1)}, bf16[768,512]{1,0:T(8,128)(2,1)}, u32[]{:S(2)}, u32[]{:S(2)}) collective-permute-start(bf16[768,512]{1,0:T(8,128)(2,1)S(1)} %slice.35.kb_ref.vb_ref.k_ref.v_ref), channel_id=1, source_target_pairs={{0,1},{1,2},{2,3},{3,4},{4,5},{5,6},{6,7},{7,8},{8,9},{9,10},{10,1... | collective-permute-start | bytes 2359304 | tf_op jit(solution)/shard_map/ppermute | solution.py:250
  134.0 63.5 %collective-permute-start.5 = (bf16[768,256]{1,0:T(8,128)(2,1)}, bf16[768,256]{1,0:T(8,128)(2,1)}, u32[]{:S(2)}, u32[]{:S(2)}) collective-permute-start(bf16[768,256]{1,0:T(8,128)(2,1)} %slice.34.q_ref), channel_id=1, source_target_pairs={{15,31},{16,0},{17,1},{18,2},{19,3},{20,4},{21,5},{22,6},{23,7},{2... | collective-permute-start | bytes 1179656 | tf_op jit(solution)/shard_map/ppermute | solution.py:249
  140.0 58.8 %collective-permute-start.9 = (bf16[768,256]{1,0:T(8,128)(2,1)}, bf16[768,256]{1,0:T(8,128)(2,1)}, u32[]{:S(2)}, u32[]{:S(2)}) collective-permute-start(bf16[768,256]{1,0:T(8,128)(2,1)} %slice.36.q_ref), channel_id=1, source_target_pairs={{15,31},{16,0},{17,1},{18,2},{19,3},{20,4},{21,5},{22,6},{23,7},{2... | collective-permute-start | bytes 1179656 | tf_op jit(solution)/shard_map/ppermute | solution.py:249
  144.1 49.0 %collective-permute-start.3 = (s32[3,6,6]{2,1,0:T(8,128)S(1)}, s32[3,6,6]{2,1,0:T(8,128)S(1)}, u32[]{:S(2)}, u32[]{:S(2)}) collective-permute-start(s32[3,6,6]{2,1,0:T(8,128)S(1)} %bitcast_select_fusion), channel_id=1, source_target_pairs={{15,31},{16,0},{17,1},{18,2},{19,3},{20,4},{21,5},{22,6},{23,7},{2... | collective-permute-start | bytes 1304 | tf_op jit(solution)/shard_map/ppermute | solution.py:239
  187.4 38.8 %all-to-all-start = ((bf16[8,96,768]{2,1,0:T(8,128)(2,1)}), bf16[8,96,768]{2,1,0:T(8,128)(2,1)S(1)}, u32[]{:S(2)}, u32[]{:S(2)}) async-start(bf16[8,96,768]{2,1,0:T(8,128)(2,1)} %pack.4), calls=%async_computation | async-start | bytes 2359296 | tf_op jit(solution)/shard_map/all_to_all | solution.py:246
  195.5 23.3 %copy-start = (bf16[768,512]{1,0:T(8,128)(2,1)}, bf16[768,512]{1,0:T(8,128)(2,1)S(1)}, u32[]{:S(2)}) copy-start(bf16[768,512]{1,0:T(8,128)(2,1)S(1)} %slice.39.kb_ref.vb_ref.k_ref.v_ref) | copy-start | bytes 2359300
  195.5 40.9 %collective-permute-start.10 = (bf16[768,512]{1,0:T(8,128)(2,1)S(1)}, bf16[768,512]{1,0:T(8,128)(2,1)}, u32[]{:S(2)}, u32[]{:S(2)}) collective-permute-start(bf16[768,512]{1,0:T(8,128)(2,1)S(1)} %slice.37.kb_ref.vb_ref.k_ref.v_ref), channel_id=1, source_target_pairs={{1,0},{2,1},{3,2},{4,3},{5,4},{6,5},{7,6},{8,7},{9,8},{10,9},{11,1... | collective-permute-start | bytes 2359304 | tf_op jit(solution)/shard_map/ppermute | solution.py:251
  197.5 40.9 %collective-permute-start.11 = (bf16[768,512]{1,0:T(8,128)(2,1)S(1)}, bf16[768,512]{1,0:T(8,128)(2,1)}, u32[]{:S(2)}, u32[]{:S(2)}) collective-permute-start(bf16[768,512]{1,0:T(8,128)(2,1)S(1)} %slice.37.kb_ref.vb_ref.k_ref.v_ref), channel_id=1, source_target_pairs={{0,1},{1,2},{2,3},{3,4},{4,5},{5,6},{6,7},{7,8},{8,9},{9,10},{10,1... | collective-permute-start | bytes 2359304 | tf_op jit(solution)/shard_map/ppermute | solution.py:250
  198.8 66.8 %collective-permute-start.14 = (bf16[768,512]{1,0:T(8,128)(2,1)S(1)}, bf16[768,512]{1,0:T(8,128)(2,1)}, u32[]{:S(2)}, u32[]{:S(2)}) collective-permute-start(bf16[768,512]{1,0:T(8,128)(2,1)S(1)} %slice.39.kb_ref.vb_ref.k_ref.v_ref), channel_id=1, source_target_pairs={{1,0},{2,1},{3,2},{4,3},{5,4},{6,5},{7,6},{8,7},{9,8},{10,9},{11,1... | collective-permute-start | bytes 2359304 | tf_op jit(solution)/shard_map/ppermute | solution.py:251
  202.8 70.3 %collective-permute-start.15 = (bf16[768,512]{1,0:T(8,128)(2,1)S(1)}, bf16[768,512]{1,0:T(8,128)(2,1)}, u32[]{:S(2)}, u32[]{:S(2)}) collective-permute-start(bf16[768,512]{1,0:T(8,128)(2,1)S(1)} %slice.39.kb_ref.vb_ref.k_ref.v_ref), channel_id=1, source_target_pairs={{0,1},{1,2},{2,3},{3,4},{4,5},{5,6},{6,7},{7,8},{8,9},{9,10},{10,1... | collective-permute-start | bytes 2359304 | tf_op jit(solution)/shard_map/ppermute | solution.py:250
  204.1 15.7 %collective-permute-start.13 = (bf16[768,256]{1,0:T(8,128)(2,1)}, bf16[768,256]{1,0:T(8,128)(2,1)S(1)}, u32[]{:S(2)}, u32[]{:S(2)}) collective-permute-start(bf16[768,256]{1,0:T(8,128)(2,1)} %slice.38.q_ref), channel_id=1, source_target_pairs={{15,31},{16,0},{17,1},{18,2},{19,3},{20,4},{21,5},{22,6},{23,7},{2... | collective-permute-start | bytes 1179656 | tf_op jit(solution)/shard_map/ppermute | solution.py:249
  219.8 6.3 %copy-start.14 = (bf16[768,256]{1,0:T(8,128)(2,1)}, bf16[768,256]{1,0:T(8,128)(2,1)S(1)}, u32[]{:S(2)}) copy-start(bf16[768,256]{1,0:T(8,128)(2,1)S(1)} %collective-permute-done.13.q_ref) | copy-start | bytes 1179652
  219.8 32.0 %collective-permute-start.8 = (bf16[792,256]{1,0:T(8,128)(2,1)}, bf16[792,256]{1,0:T(8,128)(2,1)}, u32[]{:S(2)}, u32[]{:S(2)}) collective-permute-start(bf16[792,256]{1,0:T(8,128)(2,1)} %far_attention.5), channel_id=1, source_target_pairs={{31,15},{0,16},{1,17},{2,18},{3,19},{4,20},{5,21},{6,22},{7,23},{8... | collective-permute-start | bytes 1216520 | tf_op jit(solution)/shard_map/ppermute | solution.py:253
  226.2 25.6 %copy-start.3 = (bf16[768,512]{1,0:T(8,128)(2,1)}, bf16[768,512]{1,0:T(8,128)(2,1)S(1)}, u32[]{:S(2)}) copy-start(bf16[768,512]{1,0:T(8,128)(2,1)S(1)} %slice.33.kb_ref.vb_ref.k_ref.v_ref) | copy-start | bytes 2359300
  236.4 60.5 %collective-permute-start.1 = (bf16[768,512]{1,0:T(8,128)(2,1)S(1)}, bf16[768,512]{1,0:T(8,128)(2,1)}, u32[]{:S(2)}, u32[]{:S(2)}) collective-permute-start(bf16[768,512]{1,0:T(8,128)(2,1)S(1)} %slice.33.kb_ref.vb_ref.k_ref.v_ref), channel_id=1, source_target_pairs={{1,0},{2,1},{3,2},{4,3},{5,4},{6,5},{7,6},{8,7},{9,8},{10,9},{11,1... | collective-permute-start | bytes 2359304 | tf_op jit(solution)/shard_map/ppermute | solution.py:251
  238.3 58.6 %collective-permute-start.2 = (bf16[768,512]{1,0:T(8,128)(2,1)S(1)}, bf16[768,512]{1,0:T(8,128)(2,1)S(1)}, u32[]{:S(2)}, u32[]{:S(2)}) collective-permute-start(bf16[768,512]{1,0:T(8,128)(2,1)S(1)} %slice.33.kb_ref.vb_ref.k_ref.v_ref), channel_id=1, source_target_pairs={{0,1},{1,2},{2,3},{3,4},{4,5},{5,6},{6,7},{7,8},{8,9},{9,10},{10,1... | collective-permute-start | bytes 2359304 | tf_op jit(solution)/shard_map/ppermute | solution.py:250
  251.8 35.4 %collective-permute-start.12 = (bf16[792,256]{1,0:T(8,128)(2,1)}, bf16[792,256]{1,0:T(8,128)(2,1)}, u32[]{:S(2)}, u32[]{:S(2)}) collective-permute-start(bf16[792,256]{1,0:T(8,128)(2,1)} %far_attention.6), channel_id=1, source_target_pairs={{31,15},{0,16},{1,17},{2,18},{3,19},{4,20},{5,21},{6,22},{7,23},{8... | collective-permute-start | bytes 1216520 | tf_op jit(solution)/shard_map/ppermute | solution.py:253
  258.3 33.5 %all-to-all-start.3 = ((bf16[8,96,256]{2,1,0:T(8,128)(2,1)}), bf16[8,96,256]{2,1,0:T(8,128)(2,1)}, u32[]{:S(2)}, u32[]{:S(2)}) async-start(bf16[8,96,256]{2,1,0:T(8,128)(2,1)} %bitcast.27), calls=%async_computation.3 | async-start | bytes 786432 | tf_op jit(solution)/shard_map/all_to_all | solution.py:255
  265.6 31.3 %collective-permute-start = (bf16[768,256]{1,0:T(8,128)(2,1)}, bf16[768,256]{1,0:T(8,128)(2,1)S(1)}, u32[]{:S(2)}, u32[]{:S(2)}) collective-permute-start(bf16[768,256]{1,0:T(8,128)(2,1)} %slice.32.q_ref), channel_id=1, source_target_pairs={{15,31},{16,0},{17,1},{18,2},{19,3},{20,4},{21,5},{22,6},{23,7},{2... | collective-permute-start | bytes 1179656 | tf_op jit(solution)/shard_map/ppermute | solution.py:249
  285.3 37.5 %collective-permute-start.16 = (bf16[792,256]{1,0:T(8,128)(2,1)}, bf16[792,256]{1,0:T(8,128)(2,1)S(1)}, u32[]{:S(2)}, u32[]{:S(2)}) collective-permute-start(bf16[792,256]{1,0:T(8,128)(2,1)} %far_attention.7), channel_id=1, source_target_pairs={{31,15},{0,16},{1,17},{2,18},{3,19},{4,20},{5,21},{6,22},{7,23},{8... | collective-permute-start | bytes 1216520 | tf_op jit(solution)/shard_map/ppermute | solution.py:253
  291.8 36.3 %all-to-all-start.5 = ((bf16[8,96,256]{2,1,0:T(8,128)(2,1)}), bf16[8,96,256]{2,1,0:T(8,128)(2,1)S(1)}, u32[]{:S(2)}, u32[]{:S(2)}) async-start(bf16[8,96,256]{2,1,0:T(8,128)(2,1)} %bitcast.26), calls=%async_computation.5 | async-start | bytes 786432 | tf_op jit(solution)/shard_map/all_to_all | solution.py:255
  310.8 23.3 %collective-permute-start.4 = (bf16[792,256]{1,0:T(8,128)(2,1)}, bf16[792,256]{1,0:T(8,128)(2,1)S(1)}, u32[]{:S(2)}, u32[]{:S(2)}) collective-permute-start(bf16[792,256]{1,0:T(8,128)(2,1)} %far_attention.4), channel_id=1, source_target_pairs={{31,15},{0,16},{1,17},{2,18},{3,19},{4,20},{5,21},{6,22},{7,23},{8... | collective-permute-start | bytes 1216520 | tf_op jit(solution)/shard_map/ppermute | solution.py:253
  328.1 11.3 %copy-start.9 = (bf16[8,96,256]{2,1,0:T(8,128)(2,1)}, bf16[8,96,256]{2,1,0:T(8,128)(2,1)S(1)}, u32[]{:S(2)}) copy-start(bf16[8,96,256]{2,1,0:T(8,128)(2,1)S(1)} %all-to-all-done.5.refs_0_) | copy-start | bytes 1179652
  328.1 12.6 %all-to-all-start.7 = ((bf16[8,96,256]{2,1,0:T(8,128)(2,1)}), bf16[8,96,256]{2,1,0:T(8,128)(2,1)S(1)}, u32[]{:S(2)}, u32[]{:S(2)}) async-start(bf16[8,96,256]{2,1,0:T(8,128)(2,1)} %bitcast.28), calls=%async_computation.7 | async-start | bytes 786432 | tf_op jit(solution)/shard_map/all_to_all | solution.py:255
  340.7 44.9 %all-to-all-start.1 = ((bf16[8,96,256]{2,1,0:T(8,128)(2,1)}), bf16[8,96,256]{2,1,0:T(8,128)(2,1)S(1)}, u32[]{:S(2)}, u32[]{:S(2)}) async-start(bf16[8,96,256]{2,1,0:T(8,128)(2,1)} %bitcast.29), calls=%async_computation.1 | async-start | bytes 786432 | tf_op jit(solution)/shard_map/all_to_all | solution.py:255
  (11 other events, 21.4 us)

commit v2 on v1

v2 whole, which is shorter than its diff:
```python
import functools
import math

import jax
import jax.numpy as jnp
from jax import lax
from jax.experimental import pallas as pl
from jax.experimental.pallas import tpu as pltpu
from jax.sharding import PartitionSpec as P


H = 64
HD = 128
BLOCK = 128
C = 768
QB = C // BLOCK
CHUNKS = 4
ROWS = 256
STEPS = C // ROWS
TAIL = 24
NEG = -1e30
FACTOR = HD**-0.5 * math.log2(math.e)


def eye():
    return lax.broadcasted_iota(jnp.int32, (BLOCK, BLOCK), 0) == lax.broadcasted_iota(
        jnp.int32, (BLOCK, BLOCK), 1
    )


def dot_t(a, b):
    return lax.dot_general(a, b, (((1,), (1,)), ((), ())), preferred_element_type=jnp.float32)


def far_kernel(active, q_ref, ka_ref, kb_ref, kc_ref, bias_ref, o_ref, vx_ref, lse_ref):
    step = pl.program_id(0)
    heads = q_ref.shape[1] // HD
    spans = (ka_ref, kb_ref, kc_ref)

    @pl.when(active[0] > 0)
    def _():
        @pl.when(step == 0)
        def _():
            for h in range(heads):
                for i, kv_ref in enumerate(spans):
                    vx_ref[h, i, :, :HD] = kv_ref[:, (heads + h) * HD : (heads + h + 1) * HD]
                    vx_ref[h, i, :, HD:] = jnp.ones((C, HD), jnp.bfloat16)
            lse_ref[...] = jnp.zeros_like(lse_ref)

        start = pl.multiple_of(step * ROWS, ROWS)
        for h in range(heads):
            own = slice(h * HD, (h + 1) * HD)
            q = q_ref[:, own]
            scores = []
            for i, kv_ref in enumerate(spans):
                raw = dot_t(q, kv_ref[:, own]) * FACTOR
                parts = [
                    raw[r * BLOCK : (r + 1) * BLOCK]
                    + bias_ref[pl.ds(step * (ROWS // BLOCK) + r, 1), i * C : (i + 1) * C]
                    for r in range(ROWS // BLOCK)
                ]
                scores.append(jnp.concatenate(parts, 0))
            top = functools.reduce(
                jnp.maximum, [jnp.max(s, axis=1, keepdims=True) for s in scores]
            )
            total = jnp.zeros((ROWS, 2 * HD), jnp.float32)
            for i, s in enumerate(scores):
                p = jnp.exp2(s - top).astype(jnp.bfloat16)
                total = total + jnp.dot(p, vx_ref[h, i], preferred_element_type=jnp.float32)
            sums = total[:, HD:]
            o_ref[pl.ds(start, ROWS), own] = (total[:, :HD] / sums).astype(jnp.bfloat16)
            lse = top + jnp.log2(sums)
            for r in range(ROWS // BLOCK):
                line = jnp.sum(
                    jnp.where(eye(), lse[r * BLOCK : (r + 1) * BLOCK], 0.0), axis=0, keepdims=True
                )
                lse_ref[h, pl.ds(step * (ROWS // BLOCK) + r, 1), :] = line

        @pl.when(step == STEPS - 1)
        def _():
            for h in range(heads):
                rest = lse_ref[h]
                terms = []
                for _ in range(3):
                    term = rest.astype(jnp.bfloat16).astype(jnp.float32)
                    terms.append(term)
                    rest = rest - term
                o_ref[C:, h * HD : (h + 1) * HD] = jnp.concatenate(terms, 0).astype(jnp.bfloat16)


def pack_kernel(cols, *refs):
    sources, chunks = refs[:3], refs[3:]
    for n, chunk in enumerate(chunks):
        for i, source in enumerate(sources):
            chunk[0, :, i * cols : (i + 1) * cols] = source[:, n * cols : (n + 1) * cols]


def pack(sources, groups, cols):
    rows, width = sources[0].shape
    return pl.pallas_call(
        functools.partial(pack_kernel, cols),
        out_shape=[jax.ShapeDtypeStruct((groups, rows, 3 * cols), jnp.bfloat16)] * CHUNKS,
        grid=(groups,),
        in_specs=[pl.BlockSpec((rows, width // groups), lambda g: (0, g))] * 3,
        out_specs=[pl.BlockSpec((1, rows, 3 * cols), lambda g: (g, 0, 0))] * CHUNKS,
        name="pack",
    )(*sources)


def unpack_kernel(*refs):
    pieces, whole = refs[:-1], refs[-1]
    cols = pieces[0].shape[2]
    for n, piece in enumerate(pieces):
        whole[:, n * cols : (n + 1) * cols] = piece[0]


def unpack(pieces, width):
    groups, rows, cols = pieces[0].shape
    return pl.pallas_call(
        unpack_kernel,
        out_shape=jax.ShapeDtypeStruct((rows, width), jnp.bfloat16),
        grid=(groups,),
        in_specs=[pl.BlockSpec((1, rows, cols), lambda g: (g, 0, 0))] * len(pieces),
        out_specs=pl.BlockSpec((rows, width // groups), lambda g: (0, g)),
        name="unpack",
    )(*pieces)


def far_attention(active, far_q, own, before, after, bias):
    cols = far_q.shape[1]
    heads = cols // HD
    kv = pl.BlockSpec((C, 2 * cols), lambda s, *_: (0, 0))
    return pl.pallas_call(
        far_kernel,
        out_shape=jax.ShapeDtypeStruct((C + TAIL, cols), jnp.bfloat16),
        grid_spec=pltpu.PrefetchScalarGridSpec(
            num_scalar_prefetch=1,
            grid=(STEPS,),
            in_specs=[
                pl.BlockSpec((ROWS, cols), lambda s, *_: (s, 0)),
                kv, kv, kv,
                pl.BlockSpec((8, 3 * C), lambda s, *_: (0, 0)),
            ],
            out_specs=pl.BlockSpec((C + TAIL, cols), lambda s, *_: (0, 0)),
            scratch_shapes=[
                pltpu.VMEM((heads, 3, C, 2 * HD), jnp.bfloat16),
                pltpu.VMEM((heads, 8, BLOCK), jnp.float32),
            ],
        ),
        name="far_attention",
    )(active, far_q, after, own, before, bias)


def near_kernel(receives, q_ref, kv_ref, far_ref, o_ref, vx_ref):
    heads = q_ref.shape[1] // HD
    for h in range(heads):
        own = slice(h * HD, (h + 1) * HD)
        vx_ref[h, :, :HD] = kv_ref[:, (heads + h) * HD : (heads + h + 1) * HD]
        vx_ref[h, :, HD:] = jnp.ones((C, HD), jnp.bfloat16)
        tail = far_ref[C:, own].astype(jnp.float32)
        lse_all = tail[0:8] + (tail[8:16] + tail[16:24])
        lse_all = jnp.where(receives[0] > 0, lse_all, NEG)
        for step in range(STEPS):
            lo, hi = step * ROWS, (step + 1) * ROWS
            s = dot_t(q_ref[lo:hi, own], kv_ref[:hi, own]) * FACTOR
            rows = lo + lax.broadcasted_iota(jnp.int32, (ROWS, hi), 0)
            cols = lax.broadcasted_iota(jnp.int32, (ROWS, hi), 1)
            s = jnp.where(rows >= cols, s, NEG)
            top = jnp.max(s, axis=1, keepdims=True)
            p = jnp.exp2(s - top).astype(jnp.bfloat16)
            total = jnp.dot(p, vx_ref[h, :hi, :], preferred_element_type=jnp.float32)
            columns = []
            for r in range(ROWS // BLOCK):
                line = lse_all[step * (ROWS // BLOCK) + r][None, :]
                columns.append(jnp.sum(jnp.where(eye(), line, 0.0), axis=1, keepdims=True))
            far_lse = jnp.concatenate(columns, 0)
            peak = jnp.maximum(top, far_lse)
            near_w = jnp.exp2(top - peak)
            far_w = jnp.exp2(far_lse - peak)
            far_o = far_ref[lo:hi, own].astype(jnp.float32)
            upper = total[:, :HD] * near_w + far_o * far_w
            lower = total[:, HD:] * near_w + far_w
            o_ref[lo:hi, own] = (upper / lower).astype(jnp.bfloat16)


def near_attention(receives, q, kv, far):
    cols = q.shape[1]

    def full(a):
        return pl.BlockSpec(a.shape, lambda i, *_: (0, 0))

    return pl.pallas_call(
        near_kernel,
        out_shape=jax.ShapeDtypeStruct(q.shape, jnp.bfloat16),
        grid_spec=pltpu.PrefetchScalarGridSpec(
            num_scalar_prefetch=1,
            grid=(1,),
            in_specs=[full(q), full(kv), full(far)],
            out_specs=full(q),
            scratch_shapes=[pltpu.VMEM((cols // HD, C, 2 * HD), jnp.bfloat16)],
        ),
        name="near_attention",
    )(receives, q, kv, far)


def layer(queries, keys, values, pattern):
    groups = lax.axis_size("head")
    spans = lax.axis_size("ctx")
    position = lax.axis_index("ctx")
    far = spans // 2
    tok_rows, width = queries.shape
    cols = H // groups // CHUNKS * HD
    there = [(c, (c - far) % spans) for c in range(far - 1, spans)]
    back = [(b, a) for a, b in there]
    helpers = sorted(b for _, b in there)
    from_before = [(b - 1, b) for b in helpers if b - 1 in range(far)]
    from_after = [((b + 1) % spans, b) for b in helpers]
    receives = (position >= far - 1).astype(jnp.int32)[None]
    active = ((position < far) | (position == spans - 1)).astype(jnp.int32)[None]

    distances = jnp.array([far - 1, far, far + 1], jnp.int32)
    flags = jnp.where(position >= distances[:, None, None], pattern[:, 0], 0)
    flags = lax.ppermute(flags, "ctx", there)
    lines = jnp.where(flags.transpose(1, 0, 2).reshape(QB, 3 * QB) == 1, 0.0, NEG)
    bias = jnp.repeat(jnp.pad(lines, ((0, 2), (0, 0))), BLOCK, axis=1)

    chunks = pack((queries, keys, values), groups, cols)
    pieces = []
    for packed in chunks:
        packed = lax.all_to_all(packed, "head", split_axis=0, concat_axis=0, tiled=True)
        packed = packed.reshape(C, 3 * cols)
        q, kv = packed[:, :cols], packed[:, cols:]
        far_q = lax.ppermute(q, "ctx", there)
        before = lax.ppermute(kv, "ctx", from_before)
        after = lax.ppermute(kv, "ctx", from_after)
        far_o = far_attention(active, far_q, kv, before, after, bias)
        far_o = lax.ppermute(far_o, "ctx", back)
        out = near_attention(receives, q, kv, far_o)
        out = lax.all_to_all(
            out.reshape(groups, tok_rows, cols), "head", split_axis=0, concat_axis=0, tiled=True
        )
        pieces.append(out)
    return unpack(pieces, width)


def solution(mesh):
    placed = (
        P(("ctx", "head"), None),
        P(("ctx", "head"), None),
        P(("ctx", "head"), None),
        P(None, "ctx", None, None),
    )
    return jax.shard_map(
        layer, mesh=mesh, in_specs=placed, out_specs=P(("ctx", "head"), None), check_vma=False
    )
```

time: 401 us -> 267 us (0.67)
  the two profiles are of different devices: /device:TPU:111 before, /device:TPU:198 now
where the time goes in v2:
time: 267 us; the launch traced here: 265 us
  waiting for transfers between devices  78.5 us (29%)
  starting transfers between devices  78.2 us (29%)
  blocking collectives  54.8 us (21%)
  Pallas kernels  42.6 us (16%)
  local copies, waits for them, and re-layouts  10.3 us (4%)
    ppermute x4, waiting for transfers between devices, layer(): far_o = lax.ppermute(far_o, 'ctx', back)  43.9 us
    all_to_all x2, blocking collectives, layer(): lax.all_to_all(packed, 'head', split_axis=0, concat_axis=0, tiled=True)  41.9 us
    ppermute x4, starting transfers between devices, layer(): far_q = lax.ppermute(q, 'ctx', there)  37.5 us
    ppermute x1, waiting for transfers between devices, layer(): flags = lax.ppermute(flags, 'ctx', there)  22.8 us
    pallas_call x4, Pallas kernels, near_attention(): pl.pallas_call(near_kernel, out_shape=jax.ShapeDtypeStruct(q.shape, jnp.b...  17 us
    pallas_call x4, Pallas kernels, far_attention(): pl.pallas_call(far_kernel, out_shape=jax.ShapeDtypeStruct((C + TAIL, cols...  13.5 us
    all_to_all x3, starting transfers between devices, layer(): lax.all_to_all(out.reshape(groups, tok_rows, cols), 'head', split_axis=0,...  13.3 us
    all_to_all x1, blocking collectives, layer(): lax.all_to_all(out.reshape(groups, tok_rows, cols), 'head', split_axis=0,...  13 us
  transfers between devices with their start and end apart: 22, of which 6 were waited for; matrix products, arithmetic and copies ran while one was open for 3% of the time, Pallas kernels for 12%

profile of v2, /device:TPU:198, one launch (start us, length us, event | category | flops | bytes accessed | tf_op | source)
XLA Modules:
  0.0 264.9 jit_solution(15770292612117813094)
XLA Ops:
  0.0 6.9 %pack.1 = (bf16[8,96,768]{2,1,0:T(8,128)(2,1)}, bf16[8,96,768]{2,1,0:T(8,128)(2,1)}, bf16[8,96,768]{2,1,0:T(8,128)(2,1)}, bf16[8,96,768]{2,1,0:T(8,128)(2,1)}) custom-call(bf16[96,8192]{1,0:T(8,128)(2,1)} %refs_0_.1, bf16[96,8192]{1,0:T(8,128)(2,1)} %refs_1_.1, bf16[96,8192]{1,0:T(8,128)(2,1)} %refs_2_.1), custom_call_target="tpu_custom_call" | custom-call | tf_op jit(solution)/shard_map/pack/pallas_call | solution.py:100
  6.9 22.1 %all_to_all.40 = bf16[8,96,768]{2,1,0:T(8,128)(2,1)} all-to-all(bf16[8,96,768]{2,1,0:T(8,128)(2,1)} %get-tuple-element.9), channel_id=1, replica_groups=mesh['head'=8,'ctx'=32] {'head'}, dimensions={0} | all-to-all | bytes 2359296 | tf_op jit(solution)/shard_map/all_to_all | solution.py:230
  29.0 19.8 %all_to_all.41 = bf16[8,96,768]{2,1,0:T(8,128)(2,1)S(1)} all-to-all(bf16[8,96,768]{2,1,0:T(8,128)(2,1)S(1)} %copy-done.11), channel_id=1, replica_groups=mesh['head'=8,'ctx'=32] {'head'}, dimensions={0} | all-to-all | bytes 2359296 | tf_op jit(solution)/shard_map/all_to_all | solution.py:230
  48.8 3.6 %all-to-all-start.4 = ((bf16[8,96,768]{2,1,0:T(8,128)(2,1)}), bf16[8,96,768]{2,1,0:T(8,128)(2,1)S(1)}, u32[]{:S(2)}, u32[]{:S(2)}) async-start(bf16[8,96,768]{2,1,0:T(8,128)(2,1)} %get-tuple-element.11), calls=%async_computation.4 | async-start | bytes 2359296 | tf_op jit(solution)/shard_map/all_to_all | solution.py:230
  53.6 1.7 collective-permute-start.1
  55.3 1.6 collective-permute-start.2
  56.9 1.8 slice.32.q_ref
  58.7 8.0 %collective-permute-start = (bf16[768,256]{1,0:T(8,128)(2,1)}, bf16[768,256]{1,0:T(8,128)(2,1)}, u32[]{:S(2)}, u32[]{:S(2)}) collective-permute-start(bf16[768,256]{1,0:T(8,128)(2,1)} %slice.32.q_ref), channel_id=1, source_target_pairs={{15,31},{16,0},{17,1},{18,2},{19,3},{20,4},{21,5},{22,6},{23,7},{2... | collective-permute-start | bytes 1179656 | tf_op jit(solution)/shard_map/ppermute | solution.py:233
  67.5 2.0 collective-permute-start.5
  71.9 4.7 %all-to-all-start.6 = ((bf16[8,96,768]{2,1,0:T(8,128)(2,1)}), bf16[8,96,768]{2,1,0:T(8,128)(2,1)S(1)}, u32[]{:S(2)}, u32[]{:S(2)}) async-start(bf16[8,96,768]{2,1,0:T(8,128)(2,1)} %get-tuple-element.12), calls=%async_computation.6 | async-start | bytes 2359296 | tf_op jit(solution)/shard_map/all_to_all | solution.py:230
  76.6 22.8 %collective-permute-done.3 = s32[3,6,6]{2,1,0:T(8,128)S(1)} collective-permute-done((s32[3,6,6]{2,1,0:T(8,128)S(1)}, s32[3,6,6]{2,1,0:T(8,128)S(1)}, u32[]{:S(2)}, u32[]{:S(2)}) %collective-permute-start.3) | collective-permute-done | bytes 464 | tf_op jit(solution)/shard_map/ppermute | solution.py:223
  101.9 1.6 collective-permute-start.6
  108.2 18.0 %collective-permute-start.9 = (bf16[768,256]{1,0:T(8,128)(2,1)}, bf16[768,256]{1,0:T(8,128)(2,1)S(1)}, u32[]{:S(2)}, u32[]{:S(2)}) collective-permute-start(bf16[768,256]{1,0:T(8,128)(2,1)} %slice.36.q_ref), channel_id=1, source_target_pairs={{15,31},{16,0},{17,1},{18,2},{19,3},{20,4},{21,5},{22,6},{23,7},{2... | collective-permute-start | bytes 1179656 | tf_op jit(solution)/shard_map/ppermute | solution.py:233
  126.9 3.4 %far_attention.4 = bf16[792,256]{1,0:T(8,128)(2,1)} custom-call(s32[1]{0:T(128)} %bitcast.2.active, bf16[768,256]{1,0:T(8,128)(2,1)} %collective-permute-done.q_ref, bf16[768,512]{1,0:T(8,128)(2,1)} %collective-permute-done.1.ka_ref, bf16[768,512]{1,0:T(8,128)(2,1)} %copy-done.1, bf16[768,512]{1,0:T(8,128)(2,1)} %collective-permute-done.2.kc_ref, ...), custom_call_target="tpu_custom_call" | custom-call | tf_op jit(solution)/shard_map/far_attention/pallas_call | solution.py:133
  130.3 7.9 %collective-permute-done.9.q_ref = bf16[768,256]{1,0:T(8,128)(2,1)S(1)} collective-permute-done((bf16[768,256]{1,0:T(8,128)(2,1)}, bf16[768,256]{1,0:T(8,128)(2,1)S(1)}, u32[]{:S(2)}, u32[]{:S(2)}) %collective-permute-start.9) | collective-permute-done | bytes 393248 | tf_op jit(solution)/shard_map/ppermute | solution.py:233
  142.7 3.4 %far_attention.5 = bf16[792,256]{1,0:T(8,128)(2,1)} custom-call(s32[1]{0:T(128)} %bitcast.2.active, bf16[768,256]{1,0:T(8,128)(2,1)} %collective-permute-done.5.q_ref, bf16[768,512]{1,0:T(8,128)(2,1)} %collective-permute-done.6.ka_ref, bf16[768,512]{1,0:T(8,128)(2,1)} %copy-done.2, bf16[768,512]{1,0:T(8,128)(2,1)} %collective-permute-done.7.kc_ref, ...), custom_call_target="tpu_custom_call" | custom-call | tf_op jit(solution)/shard_map/far_attention/pallas_call | solution.py:133
  146.1 22.9 %collective-permute-done.4.far_ref = bf16[792,256]{1,0:T(8,128)(2,1)} collective-permute-done((bf16[792,256]{1,0:T(8,128)(2,1)}, bf16[792,256]{1,0:T(8,128)(2,1)}, u32[]{:S(2)}, u32[]{:S(2)}) %collective-permute-start.4) | collective-permute-done | bytes 405536 | tf_op jit(solution)/shard_map/ppermute | solution.py:237
  170.3 4.2 %near_attention.4 = bf16[768,256]{1,0:T(8,128)(2,1)} custom-call(s32[1]{0:T(128)} %bitcast.receives, bf16[768,256]{1,0:T(8,128)(2,1)} %slice.32.q_ref, bf16[768,512]{1,0:T(8,128)(2,1)} %copy-done.1, bf16[792,256]{1,0:T(8,128)(2,1)} %collective-permute-done.4.far_ref), custom_call_target="tpu_custom_call" | custom-call | tf_op jit(solution)/shard_map/near_attention/pallas_call | solution.py:192
  174.5 4.4 %all-to-all-start.1 = ((bf16[8,96,256]{2,1,0:T(8,128)(2,1)}), bf16[8,96,256]{2,1,0:T(8,128)(2,1)S(1)}, u32[]{:S(2)}, u32[]{:S(2)}) async-start(bf16[8,96,256]{2,1,0:T(8,128)(2,1)} %bitcast.27), calls=%async_computation.1 | async-start | bytes 786432 | tf_op jit(solution)/shard_map/all_to_all | solution.py:239
  179.0 9.4 %collective-permute-start.13 = (bf16[768,256]{1,0:T(8,128)(2,1)S(1)}, bf16[768,256]{1,0:T(8,128)(2,1)S(1)}, u32[]{:S(2)}, u32[]{:S(2)}) collective-permute-start(bf16[768,256]{1,0:T(8,128)(2,1)S(1)} %slice.38.q_ref), channel_id=1, source_target_pairs={{15,31},{16,0},{17,1},{18,2},{19,3},{20,4},{21,5},{22,6},{23,7},{2... | collective-permute-start | bytes 1179656 | tf_op jit(solution)/shard_map/ppermute | solution.py:233
  188.4 3.4 %far_attention.6 = bf16[792,256]{1,0:T(8,128)(2,1)} custom-call(s32[1]{0:T(128)} %bitcast.2.active, bf16[768,256]{1,0:T(8,128)(2,1)} %copy-done.14, bf16[768,512]{1,0:T(8,128)(2,1)} %collective-permute-done.10.ka_ref, bf16[768,512]{1,0:T(8,128)(2,1)} %copy-done, bf16[768,512]{1,0:T(8,128)(2,1)} %collective-permute-done.11.kc_ref, ...), custom_call_target="tpu_custom_call" | custom-call | tf_op jit(solution)/shard_map/far_attention/pallas_call | solution.py:133
  193.1 12.7 %collective-permute-done.8.far_ref = bf16[792,256]{1,0:T(8,128)(2,1)} collective-permute-done((bf16[792,256]{1,0:T(8,128)(2,1)}, bf16[792,256]{1,0:T(8,128)(2,1)}, u32[]{:S(2)}, u32[]{:S(2)}) %collective-permute-start.8) | collective-permute-done | bytes 405536 | tf_op jit(solution)/shard_map/ppermute | solution.py:237
  205.8 4.3 %near_attention.5 = bf16[768,256]{1,0:T(8,128)(2,1)} custom-call(s32[1]{0:T(128)} %bitcast.receives, bf16[768,256]{1,0:T(8,128)(2,1)} %slice.34.q_ref, bf16[768,512]{1,0:T(8,128)(2,1)} %copy-done.2, bf16[792,256]{1,0:T(8,128)(2,1)} %collective-permute-done.8.far_ref), custom_call_target="tpu_custom_call" | custom-call | tf_op jit(solution)/shard_map/near_attention/pallas_call | solution.py:192
  210.0 4.4 %all-to-all-start.3 = ((bf16[8,96,256]{2,1,0:T(8,128)(2,1)}), bf16[8,96,256]{2,1,0:T(8,128)(2,1)S(1)}, u32[]{:S(2)}, u32[]{:S(2)}) async-start(bf16[8,96,256]{2,1,0:T(8,128)(2,1)} %bitcast.26), calls=%async_computation.3 | async-start | bytes 786432 | tf_op jit(solution)/shard_map/all_to_all | solution.py:239
  215.2 3.4 %far_attention.7 = bf16[792,256]{1,0:T(8,128)(2,1)} custom-call(s32[1]{0:T(128)} %bitcast.2.active, bf16[768,256]{1,0:T(8,128)(2,1)} %copy-done.15, bf16[768,512]{1,0:T(8,128)(2,1)} %collective-permute-done.14.ka_ref, bf16[768,512]{1,0:T(8,128)(2,1)} %copy-done.3, bf16[768,512]{1,0:T(8,128)(2,1)} %collective-permute-done.15.kc_ref, ...), custom_call_target="tpu_custom_call" | custom-call | tf_op jit(solution)/shard_map/far_attention/pallas_call | solution.py:133
  219.9 8.4 %collective-permute-done.12.far_ref = bf16[792,256]{1,0:T(8,128)(2,1)S(1)} collective-permute-done((bf16[792,256]{1,0:T(8,128)(2,1)}, bf16[792,256]{1,0:T(8,128)(2,1)S(1)}, u32[]{:S(2)}, u32[]{:S(2)}) %collective-permute-start.12) | collective-permute-done | bytes 405536 | tf_op jit(solution)/shard_map/ppermute | solution.py:237
  229.0 4.3 %near_attention.6 = bf16[768,256]{1,0:T(8,128)(2,1)} custom-call(s32[1]{0:T(128)} %bitcast.receives, bf16[768,256]{1,0:T(8,128)(2,1)} %slice.36.q_ref, bf16[768,512]{1,0:T(8,128)(2,1)} %copy-done, bf16[792,256]{1,0:T(8,128)(2,1)} %copy-done.12), custom_call_target="tpu_custom_call" | custom-call | tf_op jit(solution)/shard_map/near_attention/pallas_call | solution.py:192
  233.3 4.5 %all-to-all-start.5 = ((bf16[8,96,256]{2,1,0:T(8,128)(2,1)}), bf16[8,96,256]{2,1,0:T(8,128)(2,1)S(1)}, u32[]{:S(2)}, u32[]{:S(2)}) async-start(bf16[8,96,256]{2,1,0:T(8,128)(2,1)} %bitcast.28), calls=%async_computation.5 | async-start | bytes 786432 | tf_op jit(solution)/shard_map/all_to_all | solution.py:239
  238.5 4.3 %near_attention.7 = bf16[768,256]{1,0:T(8,128)(2,1)} custom-call(s32[1]{0:T(128)} %bitcast.receives, bf16[768,256]{1,0:T(8,128)(2,1)} %copy-done.10, bf16[768,512]{1,0:T(8,128)(2,1)} %copy-done.3, bf16[792,256]{1,0:T(8,128)(2,1)} %copy-done.13), custom_call_target="tpu_custom_call" | custom-call | tf_op jit(solution)/shard_map/near_attention/pallas_call | solution.py:192
  242.8 3.9 %all-to-all-done.5.refs_2_ = bf16[8,96,256]{2,1,0:T(8,128)(2,1)S(1)} async-done(((bf16[8,96,256]{2,1,0:T(8,128)(2,1)}), bf16[8,96,256]{2,1,0:T(8,128)(2,1)S(1)}, u32[]{:S(2)}, u32[]{:S(2)}) %all-to-all-start.5) | async-done | bytes 393248 | tf_op jit(solution)/shard_map/all_to_all | solution.py:239
  246.7 13.0 %all_to_all.42.refs_3_ = bf16[8,96,256]{2,1,0:T(8,128)(2,1)} all-to-all(bf16[8,96,256]{2,1,0:T(8,128)(2,1)} %bitcast.29), channel_id=1, replica_groups=mesh['head'=8,'ctx'=32] {'head'}, dimensions={0} | all-to-all | bytes 786432 | tf_op jit(solution)/shard_map/all_to_all | solution.py:239
  259.7 5.2 %unpack.1 = bf16[96,8192]{1,0:T(8,128)(2,1)} custom-call(bf16[8,96,256]{2,1,0:T(8,128)(2,1)} %copy-done.7, bf16[8,96,256]{2,1,0:T(8,128)(2,1)} %copy-done.8, bf16[8,96,256]{2,1,0:T(8,128)(2,1)} %copy-done.9, bf16[8,96,256]{2,1,0:T(8,128)(2,1)} %all_to_all.42.refs_3_), custom_call_target="tpu_custom_call" | custom-call | tf_op jit(solution)/shard_map/unpack/pallas_call | solution.py:119
  (76 shorter events, 22.8 us)
Async XLA Ops:
  6.9 22.1 %copy-start.11 = (bf16[8,96,768]{2,1,0:T(8,128)(2,1)S(1)}, bf16[8,96,768]{2,1,0:T(8,128)(2,1)}, u32[]{:S(2)}) copy-start(bf16[8,96,768]{2,1,0:T(8,128)(2,1)} %get-tuple-element.10) | copy-start | bytes 3538948
  48.8 17.9 %copy-start.6 = (bf16[8,96,768]{2,1,0:T(8,128)(2,1)}, bf16[8,96,768]{2,1,0:T(8,128)(2,1)S(1)}, u32[]{:S(2)}) copy-start(bf16[8,96,768]{2,1,0:T(8,128)(2,1)S(1)} %all_to_all.41) | copy-start | bytes 3538948
  48.8 22.1 %all-to-all-start.4 = ((bf16[8,96,768]{2,1,0:T(8,128)(2,1)}), bf16[8,96,768]{2,1,0:T(8,128)(2,1)S(1)}, u32[]{:S(2)}, u32[]{:S(2)}) async-start(bf16[8,96,768]{2,1,0:T(8,128)(2,1)} %get-tuple-element.11), calls=%async_computation.4 | async-start | bytes 2359296 | tf_op jit(solution)/shard_map/all_to_all | solution.py:230
  53.6 18.4 %copy-start.1 = (bf16[768,512]{1,0:T(8,128)(2,1)}, bf16[768,512]{1,0:T(8,128)(2,1)S(1)}, u32[]{:S(2)}) copy-start(bf16[768,512]{1,0:T(8,128)(2,1)S(1)} %slice.33.kb_ref.kv_ref) | copy-start | bytes 2359300
  53.6 15.9 %copy-start.16 = (s32[3,1,6,6]{3,1,2,0:T(1,128)S(1)}, s32[3,1,6,6]{3,1,2,0:T(1,128)}, u32[]{:S(2)}) copy-start(s32[3,1,6,6]{3,1,2,0:T(1,128)} %param.8) | copy-start | bytes 1300
  53.6 53.0 %collective-permute-start.1 = (bf16[768,512]{1,0:T(8,128)(2,1)S(1)}, bf16[768,512]{1,0:T(8,128)(2,1)}, u32[]{:S(2)}, u32[]{:S(2)}) collective-permute-start(bf16[768,512]{1,0:T(8,128)(2,1)S(1)} %slice.33.kb_ref.kv_ref), channel_id=1, source_target_pairs={{1,0},{2,1},{3,2},{4,3},{5,4},{6,5},{7,6},{8,7},{9,8},{10,9},{11,1... | collective-permute-start | bytes 2359304 | tf_op jit(solution)/shard_map/ppermute | solution.py:235
  55.3 52.9 %collective-permute-start.2 = (bf16[768,512]{1,0:T(8,128)(2,1)S(1)}, bf16[768,512]{1,0:T(8,128)(2,1)}, u32[]{:S(2)}, u32[]{:S(2)}) collective-permute-start(bf16[768,512]{1,0:T(8,128)(2,1)S(1)} %slice.33.kb_ref.kv_ref), channel_id=1, source_target_pairs={{0,1},{1,2},{2,3},{3,4},{4,5},{5,6},{6,7},{7,8},{8,9},{9,10},{10,1... | collective-permute-start | bytes 2359304 | tf_op jit(solution)/shard_map/ppermute | solution.py:234
  58.7 44.8 %collective-permute-start = (bf16[768,256]{1,0:T(8,128)(2,1)}, bf16[768,256]{1,0:T(8,128)(2,1)}, u32[]{:S(2)}, u32[]{:S(2)}) collective-permute-start(bf16[768,256]{1,0:T(8,128)(2,1)} %slice.32.q_ref), channel_id=1, source_target_pairs={{15,31},{16,0},{17,1},{18,2},{19,3},{20,4},{21,5},{22,6},{23,7},{2... | collective-permute-start | bytes 1179656 | tf_op jit(solution)/shard_map/ppermute | solution.py:233
  67.5 37.6 %collective-permute-start.5 = (bf16[768,256]{1,0:T(8,128)(2,1)}, bf16[768,256]{1,0:T(8,128)(2,1)}, u32[]{:S(2)}, u32[]{:S(2)}) collective-permute-start(bf16[768,256]{1,0:T(8,128)(2,1)} %slice.34.q_ref), channel_id=1, source_target_pairs={{15,31},{16,0},{17,1},{18,2},{19,3},{20,4},{21,5},{22,6},{23,7},{2... | collective-permute-start | bytes 1179656 | tf_op jit(solution)/shard_map/ppermute | solution.py:233
  69.6 29.8 %collective-permute-start.3 = (s32[3,6,6]{2,1,0:T(8,128)S(1)}, s32[3,6,6]{2,1,0:T(8,128)S(1)}, u32[]{:S(2)}, u32[]{:S(2)}) collective-permute-start(s32[3,6,6]{2,1,0:T(8,128)S(1)} %bitcast_select_fusion), channel_id=1, source_target_pairs={{15,31},{16,0},{17,1},{18,2},{19,3},{20,4},{21,5},{22,6},{23,7},{2... | collective-permute-start | bytes 1304 | tf_op jit(solution)/shard_map/ppermute | solution.py:223
  71.9 67.5 %all-to-all-start.6 = ((bf16[8,96,768]{2,1,0:T(8,128)(2,1)}), bf16[8,96,768]{2,1,0:T(8,128)(2,1)S(1)}, u32[]{:S(2)}, u32[]{:S(2)}) async-start(bf16[8,96,768]{2,1,0:T(8,128)(2,1)} %get-tuple-element.12), calls=%async_computation.6 | async-start | bytes 2359296 | tf_op jit(solution)/shard_map/all_to_all | solution.py:230
  101.9 28.4 %copy-start = (bf16[768,512]{1,0:T(8,128)(2,1)}, bf16[768,512]{1,0:T(8,128)(2,1)S(1)}, u32[]{:S(2)}) copy-start(bf16[768,512]{1,0:T(8,128)(2,1)S(1)} %slice.37.kb_ref.kv_ref) | copy-start | bytes 2359300
  101.9 37.7 %collective-permute-start.6 = (bf16[768,512]{1,0:T(8,128)(2,1)S(1)}, bf16[768,512]{1,0:T(8,128)(2,1)}, u32[]{:S(2)}, u32[]{:S(2)}) collective-permute-start(bf16[768,512]{1,0:T(8,128)(2,1)S(1)} %slice.35.kb_ref.kv_ref), channel_id=1, source_target_pairs={{1,0},{2,1},{3,2},{4,3},{5,4},{6,5},{7,6},{8,7},{9,8},{10,9},{11,1... | collective-permute-start | bytes 2359304 | tf_op jit(solution)/shard_map/ppermute | solution.py:235
  103.5 37.6 %collective-permute-start.7 = (bf16[768,512]{1,0:T(8,128)(2,1)S(1)}, bf16[768,512]{1,0:T(8,128)(2,1)}, u32[]{:S(2)}, u32[]{:S(2)}) collective-permute-start(bf16[768,512]{1,0:T(8,128)(2,1)S(1)} %slice.35.kb_ref.kv_ref), channel_id=1, source_target_pairs={{0,1},{1,2},{2,3},{3,4},{4,5},{5,6},{6,7},{7,8},{8,9},{9,10},{10,1... | collective-permute-start | bytes 2359304 | tf_op jit(solution)/shard_map/ppermute | solution.py:234
  105.1 73.9 %collective-permute-start.10 = (bf16[768,512]{1,0:T(8,128)(2,1)S(1)}, bf16[768,512]{1,0:T(8,128)(2,1)}, u32[]{:S(2)}, u32[]{:S(2)}) collective-permute-start(bf16[768,512]{1,0:T(8,128)(2,1)S(1)} %slice.37.kb_ref.kv_ref), channel_id=1, source_target_pairs={{1,0},{2,1},{3,2},{4,3},{5,4},{6,5},{7,6},{8,7},{9,8},{10,9},{11,1... | collective-permute-start | bytes 2359304 | tf_op jit(solution)/shard_map/ppermute | solution.py:235
  106.6 81.8 %collective-permute-start.11 = (bf16[768,512]{1,0:T(8,128)(2,1)S(1)}, bf16[768,512]{1,0:T(8,128)(2,1)}, u32[]{:S(2)}, u32[]{:S(2)}) collective-permute-start(bf16[768,512]{1,0:T(8,128)(2,1)S(1)} %slice.37.kb_ref.kv_ref), channel_id=1, source_target_pairs={{0,1},{1,2},{2,3},{3,4},{4,5},{5,6},{6,7},{7,8},{8,9},{9,10},{10,1... | collective-permute-start | bytes 2359304 | tf_op jit(solution)/shard_map/ppermute | solution.py:234
  108.2 30.0 %collective-permute-start.9 = (bf16[768,256]{1,0:T(8,128)(2,1)}, bf16[768,256]{1,0:T(8,128)(2,1)S(1)}, u32[]{:S(2)}, u32[]{:S(2)}) collective-permute-start(bf16[768,256]{1,0:T(8,128)(2,1)} %slice.36.q_ref), channel_id=1, source_target_pairs={{15,31},{16,0},{17,1},{18,2},{19,3},{20,4},{21,5},{22,6},{23,7},{2... | collective-permute-start | bytes 1179656 | tf_op jit(solution)/shard_map/ppermute | solution.py:233
  138.2 30.8 %collective-permute-start.4 = (bf16[792,256]{1,0:T(8,128)(2,1)}, bf16[792,256]{1,0:T(8,128)(2,1)}, u32[]{:S(2)}, u32[]{:S(2)}) collective-permute-start(bf16[792,256]{1,0:T(8,128)(2,1)} %far_attention.4), channel_id=1, source_target_pairs={{31,15},{0,16},{1,17},{2,18},{3,19},{4,20},{5,21},{6,22},{7,23},{8... | collective-permute-start | bytes 1216520 | tf_op jit(solution)/shard_map/ppermute | solution.py:237
  139.6 6.5 %copy-start.3 = (bf16[768,512]{1,0:T(8,128)(2,1)}, bf16[768,512]{1,0:T(8,128)(2,1)S(1)}, u32[]{:S(2)}) copy-start(bf16[768,512]{1,0:T(8,128)(2,1)S(1)} %slice.39.kb_ref.kv_ref) | copy-start | bytes 2359300
  139.6 74.9 %collective-permute-start.14 = (bf16[768,512]{1,0:T(8,128)(2,1)S(1)}, bf16[768,512]{1,0:T(8,128)(2,1)}, u32[]{:S(2)}, u32[]{:S(2)}) collective-permute-start(bf16[768,512]{1,0:T(8,128)(2,1)S(1)} %slice.39.kb_ref.kv_ref), channel_id=1, source_target_pairs={{1,0},{2,1},{3,2},{4,3},{5,4},{6,5},{7,6},{8,7},{9,8},{10,9},{11,1... | collective-permute-start | bytes 2359304 | tf_op jit(solution)/shard_map/ppermute | solution.py:235
  141.1 73.4 %collective-permute-start.15 = (bf16[768,512]{1,0:T(8,128)(2,1)S(1)}, bf16[768,512]{1,0:T(8,128)(2,1)}, u32[]{:S(2)}, u32[]{:S(2)}) collective-permute-start(bf16[768,512]{1,0:T(8,128)(2,1)S(1)} %slice.39.kb_ref.kv_ref), channel_id=1, source_target_pairs={{0,1},{1,2},{2,3},{3,4},{4,5},{5,6},{6,7},{7,8},{8,9},{9,10},{10,1... | collective-permute-start | bytes 2359304 | tf_op jit(solution)/shard_map/ppermute | solution.py:234
  169.0 36.8 %collective-permute-start.8 = (bf16[792,256]{1,0:T(8,128)(2,1)}, bf16[792,256]{1,0:T(8,128)(2,1)}, u32[]{:S(2)}, u32[]{:S(2)}) collective-permute-start(bf16[792,256]{1,0:T(8,128)(2,1)} %far_attention.5), channel_id=1, source_target_pairs={{31,15},{0,16},{1,17},{2,18},{3,19},{4,20},{5,21},{6,22},{7,23},{8... | collective-permute-start | bytes 1216520 | tf_op jit(solution)/shard_map/ppermute | solution.py:237
  174.5 35.5 %all-to-all-start.1 = ((bf16[8,96,256]{2,1,0:T(8,128)(2,1)}), bf16[8,96,256]{2,1,0:T(8,128)(2,1)S(1)}, u32[]{:S(2)}, u32[]{:S(2)}) async-start(bf16[8,96,256]{2,1,0:T(8,128)(2,1)} %bitcast.27), calls=%async_computation.1 | async-start | bytes 786432 | tf_op jit(solution)/shard_map/all_to_all | solution.py:239
  179.0 12.8 %copy-start.10 = (bf16[768,256]{1,0:T(8,128)(2,1)}, bf16[768,256]{1,0:T(8,128)(2,1)S(1)}, u32[]{:S(2)}) copy-start(bf16[768,256]{1,0:T(8,128)(2,1)S(1)} %slice.38.q_ref) | copy-start | bytes 1179652
  179.0 35.5 %collective-permute-start.13 = (bf16[768,256]{1,0:T(8,128)(2,1)S(1)}, bf16[768,256]{1,0:T(8,128)(2,1)S(1)}, u32[]{:S(2)}, u32[]{:S(2)}) collective-permute-start(bf16[768,256]{1,0:T(8,128)(2,1)S(1)} %slice.38.q_ref), channel_id=1, source_target_pairs={{15,31},{16,0},{17,1},{18,2},{19,3},{20,4},{21,5},{22,6},{23,7},{2... | collective-permute-start | bytes 1179656 | tf_op jit(solution)/shard_map/ppermute | solution.py:233
  191.8 36.5 %collective-permute-start.12 = (bf16[792,256]{1,0:T(8,128)(2,1)}, bf16[792,256]{1,0:T(8,128)(2,1)S(1)}, u32[]{:S(2)}, u32[]{:S(2)}) collective-permute-start(bf16[792,256]{1,0:T(8,128)(2,1)} %far_attention.6), channel_id=1, source_target_pairs={{31,15},{0,16},{1,17},{2,18},{3,19},{4,20},{5,21},{6,22},{7,23},{8... | collective-permute-start | bytes 1216520 | tf_op jit(solution)/shard_map/ppermute | solution.py:237
  210.0 8.6 %copy-start.7 = (bf16[8,96,256]{2,1,0:T(8,128)(2,1)}, bf16[8,96,256]{2,1,0:T(8,128)(2,1)S(1)}, u32[]{:S(2)}) copy-start(bf16[8,96,256]{2,1,0:T(8,128)(2,1)S(1)} %all-to-all-done.1.refs_0_) | copy-start | bytes 1179652
  210.0 23.2 %all-to-all-start.3 = ((bf16[8,96,256]{2,1,0:T(8,128)(2,1)}), bf16[8,96,256]{2,1,0:T(8,128)(2,1)S(1)}, u32[]{:S(2)}, u32[]{:S(2)}) async-start(bf16[8,96,256]{2,1,0:T(8,128)(2,1)} %bitcast.26), calls=%async_computation.3 | async-start | bytes 786432 | tf_op jit(solution)/shard_map/all_to_all | solution.py:239
  218.6 19.2 %collective-permute-start.16 = (bf16[792,256]{1,0:T(8,128)(2,1)}, bf16[792,256]{1,0:T(8,128)(2,1)S(1)}, u32[]{:S(2)}, u32[]{:S(2)}) collective-permute-start(bf16[792,256]{1,0:T(8,128)(2,1)} %far_attention.7), channel_id=1, source_target_pairs={{31,15},{0,16},{1,17},{2,18},{3,19},{4,20},{5,21},{6,22},{7,23},{8... | collective-permute-start | bytes 1216520 | tf_op jit(solution)/shard_map/ppermute | solution.py:237
  233.3 9.5 %copy-start.8 = (bf16[8,96,256]{2,1,0:T(8,128)(2,1)}, bf16[8,96,256]{2,1,0:T(8,128)(2,1)S(1)}, u32[]{:S(2)}) copy-start(bf16[8,96,256]{2,1,0:T(8,128)(2,1)S(1)} %all-to-all-done.3.refs_1_) | copy-start | bytes 1179652
  233.3 13.4 %all-to-all-start.5 = ((bf16[8,96,256]{2,1,0:T(8,128)(2,1)}), bf16[8,96,256]{2,1,0:T(8,128)(2,1)S(1)}, u32[]{:S(2)}, u32[]{:S(2)}) async-start(bf16[8,96,256]{2,1,0:T(8,128)(2,1)} %bitcast.28), calls=%async_computation.5 | async-start | bytes 786432 | tf_op jit(solution)/shard_map/all_to_all | solution.py:239
  246.7 13.0 %copy-start.9 = (bf16[8,96,256]{2,1,0:T(8,128)(2,1)}, bf16[8,96,256]{2,1,0:T(8,128)(2,1)S(1)}, u32[]{:S(2)}) copy-start(bf16[8,96,256]{2,1,0:T(8,128)(2,1)S(1)} %all-to-all-done.5.refs_2_) | copy-start | bytes 1179652
  (8 other events, 13.4 us)

commit v3 on v2

--- a/solution.py
+++ b/solution.py
@@ -14,7 +14,8 @@
 BLOCK = 128
 C = 768
 QB = C // BLOCK
-CHUNKS = 4
+MODES = ("q", "kv", "q", "q")
+CHUNKS = len(MODES)
 ROWS = 256
 STEPS = C // ROWS
 TAIL = 24
@@ -177,7 +178,7 @@
             peak = jnp.maximum(top, far_lse)
             near_w = jnp.exp2(top - peak)
             far_w = jnp.exp2(far_lse - peak)
-            far_o = far_ref[lo:hi, own].astype(jnp.float32)
+            far_o = jnp.where(receives[0] > 0, far_ref[lo:hi, own].astype(jnp.float32), 0.0)
             upper = total[:, :HD] * near_w + far_o * far_w
             lower = total[:, HD:] * near_w + far_w
             o_ref[lo:hi, own] = (upper / lower).astype(jnp.bfloat16)
@@ -215,26 +216,41 @@
     helpers = sorted(b for _, b in there)
     from_before = [(b - 1, b) for b in helpers if b - 1 in range(far)]
     from_after = [((b + 1) % spans, b) for b in helpers]
-    receives = (position >= far - 1).astype(jnp.int32)[None]
+    ahead = [(s, (s + far) % spans) for s in range(far + 1)]
+    readers = range(far - 1, spans)
+    pass_before = [(c - 1, c) for c in readers if c > far]
+    pass_after = [((c + 1) % spans, c) for c in readers]
+    reads_far = position >= far - 1
+    receives = reads_far.astype(jnp.int32)[None]
     active = ((position < far) | (position == spans - 1)).astype(jnp.int32)[None]
 
     distances = jnp.array([far - 1, far, far + 1], jnp.int32)
     flags = jnp.where(position >= distances[:, None, None], pattern[:, 0], 0)
-    flags = lax.ppermute(flags, "ctx", there)
-    lines = jnp.where(flags.transpose(1, 0, 2).reshape(QB, 3 * QB) == 1, 0.0, NEG)
-    bias = jnp.repeat(jnp.pad(lines, ((0, 2), (0, 0))), BLOCK, axis=1)
+
+    def bias_of(flags):
+        lines = jnp.where(flags.transpose(1, 0, 2).reshape(QB, 3 * QB) == 1, 0.0, NEG)
+        return jnp.repeat(jnp.pad(lines, ((0, 2), (0, 0))), BLOCK, axis=1)
+
+    own_bias = bias_of(flags)
+    bias = bias_of(lax.ppermute(flags, "ctx", there))
 
     chunks = pack((queries, keys, values), groups, cols)
     pieces = []
-    for packed in chunks:
+    for n, packed in enumerate(chunks):
         packed = lax.all_to_all(packed, "head", split_axis=0, concat_axis=0, tiled=True)
         packed = packed.reshape(C, 3 * cols)
         q, kv = packed[:, :cols], packed[:, cols:]
-        far_q = lax.ppermute(q, "ctx", there)
-        before = lax.ppermute(kv, "ctx", from_before)
-        after = lax.ppermute(kv, "ctx", from_after)
-        far_o = far_attention(active, far_q, kv, before, after, bias)
-        far_o = lax.ppermute(far_o, "ctx", back)
+        if MODES[n] == "kv":
+            shipped = lax.ppermute(kv, "ctx", ahead)
+            before = lax.ppermute(shipped, "ctx", pass_before)
+            after = lax.ppermute(shipped, "ctx", pass_after)
+            far_o = far_attention(receives, q, shipped, before, after, own_bias)
+        else:
+            far_q = lax.ppermute(q, "ctx", there)
+            before = lax.ppermute(kv, "ctx", from_before)
+            after = lax.ppermute(kv, "ctx", from_after)
+            far_o = far_attention(active, far_q, kv, before, after, bias)
+            far_o = lax.ppermute(far_o, "ctx", back)
         out = near_attention(receives, q, kv, far_o)
         out = lax.all_to_all(
             out.reshape(groups, tok_rows, cols), "head", split_axis=0, concat_axis=0, tiled=True

time: 267 us -> 285 us (1.067)
  the two profiles are of different devices: /device:TPU:198 before, /device:TPU:192 now
where the time goes in v3:
time: 285 us; the launch traced here: 283 us
  starting transfers between devices  88.7 us (31%)
  waiting for transfers between devices  78.6 us (28%)
  blocking collectives  55.9 us (20%)
  Pallas kernels  48.8 us (17%)
  local copies, waits for them, and re-layouts  10.7 us (4%)
    ppermute x3, waiting for transfers between devices, layer(): far_o = lax.ppermute(far_o, 'ctx', back)  50.5 us
    all_to_all x2, blocking collectives, layer(): lax.all_to_all(packed, 'head', split_axis=0, concat_axis=0, tiled=True)  42.5 us
    ppermute x3, starting transfers between devices, layer(): far_q = lax.ppermute(q, 'ctx', there)  33 us
    pallas_call x4, Pallas kernels, far_attention(): pl.pallas_call(far_kernel, out_shape=jax.ShapeDtypeStruct((C + TAIL, cols...  19.6 us
    ppermute x1, starting transfers between devices, layer(): after = lax.ppermute(shipped, 'ctx', pass_after)  18.2 us
    pallas_call x4, Pallas kernels, near_attention(): pl.pallas_call(near_kernel, out_shape=jax.ShapeDtypeStruct(q.shape, jnp.b...  17.1 us
    all_to_all x1, blocking collectives, layer(): lax.all_to_all(out.reshape(groups, tok_rows, cols), 'head', split_axis=0,...  13.4 us
    all_to_all x3, starting transfers between devices, layer(): lax.all_to_all(out.reshape(groups, tok_rows, cols), 'head', split_axis=0,...  12.4 us
  transfers between devices with their start and end apart: 21, of which 7 were waited for; matrix products, arithmetic and copies ran while one was open for 3% of the time, Pallas kernels for 13%

profile of v3, /device:TPU:192, one launch (start us, length us, event | category | flops | bytes accessed | tf_op | source)
XLA Modules:
  0.0 283.3 jit_solution(15981667452748642027)
XLA Ops:
  0.0 6.9 %pack.1 = (bf16[8,96,768]{2,1,0:T(8,128)(2,1)}, bf16[8,96,768]{2,1,0:T(8,128)(2,1)}, bf16[8,96,768]{2,1,0:T(8,128)(2,1)}, bf16[8,96,768]{2,1,0:T(8,128)(2,1)}) custom-call(bf16[96,8192]{1,0:T(8,128)(2,1)} %refs_0_.1, bf16[96,8192]{1,0:T(8,128)(2,1)} %refs_1_.1, bf16[96,8192]{1,0:T(8,128)(2,1)} %refs_2_.1), custom_call_target="tpu_custom_call" | custom-call | tf_op jit(solution)/shard_map/pack/pallas_call | solution.py:101
  6.9 22.0 %all_to_all.40 = bf16[8,96,768]{2,1,0:T(8,128)(2,1)S(1)} all-to-all(bf16[8,96,768]{2,1,0:T(8,128)(2,1)} %get-tuple-element.9), channel_id=1, replica_groups=mesh['head'=8,'ctx'=32] {'head'}, dimensions={0} | all-to-all | bytes 2359296 | tf_op jit(solution)/shard_map/all_to_all | solution.py:240
  28.9 20.5 %all_to_all.41 = bf16[8,96,768]{2,1,0:T(8,128)(2,1)} all-to-all(bf16[8,96,768]{2,1,0:T(8,128)(2,1)S(1)} %copy-done.9), channel_id=1, replica_groups=mesh['head'=8,'ctx'=32] {'head'}, dimensions={0} | all-to-all | bytes 2359296 | tf_op jit(solution)/shard_map/all_to_all | solution.py:240
  49.4 3.6 %all-to-all-start.6 = ((bf16[8,96,768]{2,1,0:T(8,128)(2,1)}), bf16[8,96,768]{2,1,0:T(8,128)(2,1)S(1)}, u32[]{:S(2)}, u32[]{:S(2)}) async-start(bf16[8,96,768]{2,1,0:T(8,128)(2,1)} %get-tuple-element.12), calls=%async_computation.6 | async-start | bytes 2359296 | tf_op jit(solution)/shard_map/all_to_all | solution.py:240
  57.0 6.2 %collective-permute-start = (bf16[768,256]{1,0:T(8,128)(2,1)}, bf16[768,256]{1,0:T(8,128)(2,1)}, u32[]{:S(2)}, u32[]{:S(2)}) collective-permute-start(bf16[768,256]{1,0:T(8,128)(2,1)} %slice.32.q_ref), channel_id=1, source_target_pairs={{15,31},{16,0},{17,1},{18,2},{19,3},{20,4},{21,5},{22,6},{23,7},{2... | collective-permute-start | bytes 1179656 | tf_op jit(solution)/shard_map/ppermute | solution.py:249
  64.6 5.6 %all-to-all-done.6 = bf16[8,96,768]{2,1,0:T(8,128)(2,1)S(1)} async-done(((bf16[8,96,768]{2,1,0:T(8,128)(2,1)}), bf16[8,96,768]{2,1,0:T(8,128)(2,1)S(1)}, u32[]{:S(2)}, u32[]{:S(2)}) %all-to-all-start.6) | async-done | bytes 1179680 | tf_op jit(solution)/shard_map/all_to_all | solution.py:240
  71.3 3.6 %all-to-all-start.2 = ((bf16[8,96,768]{2,1,0:T(8,128)(2,1)}), bf16[8,96,768]{2,1,0:T(8,128)(2,1)S(1)}, u32[]{:S(2)}, u32[]{:S(2)}) async-start(bf16[8,96,768]{2,1,0:T(8,128)(2,1)} %get-tuple-element.10), calls=%async_computation.2 | async-start | bytes 2359296 | tf_op jit(solution)/shard_map/all_to_all | solution.py:240
  74.8 5.4 %collective-permute-done.3 = s32[3,6,6]{2,1,0:T(8,128)S(1)} collective-permute-done((s32[3,6,6]{2,1,0:T(8,128)S(1)}, s32[3,6,6]{2,1,0:T(8,128)S(1)}, u32[]{:S(2)}, u32[]{:S(2)}) %collective-permute-start.3) | collective-permute-done | bytes 464 | tf_op jit(solution)/shard_map/ppermute | solution.py:235
  80.4 1.9 slice.36.q_ref
  89.9 16.7 %collective-permute-start.8 = (bf16[768,256]{1,0:T(8,128)(2,1)}, bf16[768,256]{1,0:T(8,128)(2,1)S(1)}, u32[]{:S(2)}, u32[]{:S(2)}) collective-permute-start(bf16[768,256]{1,0:T(8,128)(2,1)} %slice.36.q_ref), channel_id=1, source_target_pairs={{15,31},{16,0},{17,1},{18,2},{19,3},{20,4},{21,5},{22,6},{23,7},{2... | collective-permute-start | bytes 1179656 | tf_op jit(solution)/shard_map/ppermute | solution.py:249
  107.3 3.4 %far_attention.4 = bf16[792,256]{1,0:T(8,128)(2,1)} custom-call(s32[1]{0:T(128)} %bitcast.2.active, bf16[768,256]{1,0:T(8,128)(2,1)} %collective-permute-done.q_ref, bf16[768,512]{1,0:T(8,128)(2,1)} %collective-permute-done.1.ka_ref, bf16[768,512]{1,0:T(8,128)(2,1)} %copy-done, bf16[768,512]{1,0:T(8,128)(2,1)} %collective-permute-done.2.kc_ref, ...), custom_call_target="tpu_custom_call" | custom-call | tf_op jit(solution)/shard_map/far_attention/pallas_call | solution.py:134
  110.7 6.6 %collective-permute-done.8.q_ref = bf16[768,256]{1,0:T(8,128)(2,1)S(1)} collective-permute-done((bf16[768,256]{1,0:T(8,128)(2,1)}, bf16[768,256]{1,0:T(8,128)(2,1)S(1)}, u32[]{:S(2)}, u32[]{:S(2)}) %collective-permute-start.8) | collective-permute-done | bytes 393248 | tf_op jit(solution)/shard_map/ppermute | solution.py:249
  120.0 1.8 slice.38.q_ref
  121.7 10.1 %collective-permute-start.12 = (bf16[768,256]{1,0:T(8,128)(2,1)}, bf16[768,256]{1,0:T(8,128)(2,1)S(1)}, u32[]{:S(2)}, u32[]{:S(2)}) collective-permute-start(bf16[768,256]{1,0:T(8,128)(2,1)} %slice.38.q_ref), channel_id=1, source_target_pairs={{15,31},{16,0},{17,1},{18,2},{19,3},{20,4},{21,5},{22,6},{23,7},{2... | collective-permute-start | bytes 1179656 | tf_op jit(solution)/shard_map/ppermute | solution.py:249
  131.9 3.4 %far_attention.6 = bf16[792,256]{1,0:T(8,128)(2,1)} custom-call(s32[1]{0:T(128)} %bitcast.2.active, bf16[768,256]{1,0:T(8,128)(2,1)} %copy-done.12, bf16[768,512]{1,0:T(8,128)(2,1)} %collective-permute-done.9.ka_ref, bf16[768,512]{1,0:T(8,128)(2,1)} %copy-done.2, bf16[768,512]{1,0:T(8,128)(2,1)} %collective-permute-done.10.kc_ref, ...), custom_call_target="tpu_custom_call" | custom-call | tf_op jit(solution)/shard_map/far_attention/pallas_call | solution.py:134
  135.2 15.4 %collective-permute-done.4.far_ref = bf16[792,256]{1,0:T(8,128)(2,1)} collective-permute-done((bf16[792,256]{1,0:T(8,128)(2,1)}, bf16[792,256]{1,0:T(8,128)(2,1)}, u32[]{:S(2)}, u32[]{:S(2)}) %collective-permute-start.4) | collective-permute-done | bytes 405536 | tf_op jit(solution)/shard_map/ppermute | solution.py:253
  151.9 4.3 %near_attention.4 = bf16[768,256]{1,0:T(8,128)(2,1)} custom-call(s32[1]{0:T(128)} %bitcast.receives.active, bf16[768,256]{1,0:T(8,128)(2,1)} %slice.32.q_ref, bf16[768,512]{1,0:T(8,128)(2,1)} %copy-done, bf16[792,256]{1,0:T(8,128)(2,1)} %collective-permute-done.4.far_ref), custom_call_target="tpu_custom_call" | custom-call | tf_op jit(solution)/shard_map/near_attention/pallas_call | solution.py:193
  156.2 3.6 %all-to-all-start.1 = ((bf16[8,96,256]{2,1,0:T(8,128)(2,1)}), bf16[8,96,256]{2,1,0:T(8,128)(2,1)S(1)}, u32[]{:S(2)}, u32[]{:S(2)}) async-start(bf16[8,96,256]{2,1,0:T(8,128)(2,1)} %bitcast.35), calls=%async_computation.1 | async-start | bytes 786432 | tf_op jit(solution)/shard_map/all_to_all | solution.py:255
  160.6 3.4 %far_attention.7 = bf16[792,256]{1,0:T(8,128)(2,1)} custom-call(s32[1]{0:T(128)} %bitcast.2.active, bf16[768,256]{1,0:T(8,128)(2,1)} %copy-done.11, bf16[768,512]{1,0:T(8,128)(2,1)} %collective-permute-done.13.ka_ref, bf16[768,512]{1,0:T(8,128)(2,1)} %copy-done.1, bf16[768,512]{1,0:T(8,128)(2,1)} %collective-permute-done.14.kc_ref, ...), custom_call_target="tpu_custom_call" | custom-call | tf_op jit(solution)/shard_map/far_attention/pallas_call | solution.py:134
  165.3 35.1 %collective-permute-done.11.far_ref = bf16[792,256]{1,0:T(8,128)(2,1)} collective-permute-done((bf16[792,256]{1,0:T(8,128)(2,1)}, bf16[792,256]{1,0:T(8,128)(2,1)}, u32[]{:S(2)}, u32[]{:S(2)}) %collective-permute-start.11) | collective-permute-done | bytes 405536 | tf_op jit(solution)/shard_map/ppermute | solution.py:253
  200.4 4.3 %near_attention.6 = bf16[768,256]{1,0:T(8,128)(2,1)} custom-call(s32[1]{0:T(128)} %bitcast.receives.active, bf16[768,256]{1,0:T(8,128)(2,1)} %slice.36.q_ref, bf16[768,512]{1,0:T(8,128)(2,1)} %copy-done.2, bf16[792,256]{1,0:T(8,128)(2,1)} %collective-permute-done.11.far_ref), custom_call_target="tpu_custom_call" | custom-call | tf_op jit(solution)/shard_map/near_attention/pallas_call | solution.py:193
  204.7 3.9 %all-to-all-start.5 = ((bf16[8,96,256]{2,1,0:T(8,128)(2,1)}), bf16[8,96,256]{2,1,0:T(8,128)(2,1)S(1)}, u32[]{:S(2)}, u32[]{:S(2)}) async-start(bf16[8,96,256]{2,1,0:T(8,128)(2,1)} %bitcast.34), calls=%async_computation.5 | async-start | bytes 786432 | tf_op jit(solution)/shard_map/all_to_all | solution.py:255
  208.6 18.2 %collective-permute-start.6 = (bf16[768,512]{1,0:T(8,128)(2,1)}, bf16[768,512]{1,0:T(8,128)(2,1)}, u32[]{:S(2)}, u32[]{:S(2)}) collective-permute-start(bf16[768,512]{1,0:T(8,128)(2,1)} %collective-permute-done.5.kb_ref), channel_id=1, source_target_pairs={{16,15},{17,16},{18,17},{19,18},{20,19},{21,20},{22,21},{23,22},{2... | collective-permute-start | bytes 2359304 | tf_op jit(solution)/shard_map/ppermute | solution.py:246
  226.9 1.9 collective-permute-start.7
  229.8 4.3 %near_attention.7 = bf16[768,256]{1,0:T(8,128)(2,1)} custom-call(s32[1]{0:T(128)} %bitcast.receives.active, bf16[768,256]{1,0:T(8,128)(2,1)} %slice.38.q_ref, bf16[768,512]{1,0:T(8,128)(2,1)} %copy-done.1, bf16[792,256]{1,0:T(8,128)(2,1)} %copy-done.10), custom_call_target="tpu_custom_call" | custom-call | tf_op jit(solution)/shard_map/near_attention/pallas_call | solution.py:193
  234.1 4.8 %all-to-all-start.7 = ((bf16[8,96,256]{2,1,0:T(8,128)(2,1)}), bf16[8,96,256]{2,1,0:T(8,128)(2,1)S(1)}, u32[]{:S(2)}, u32[]{:S(2)}) async-start(bf16[8,96,256]{2,1,0:T(8,128)(2,1)} %bitcast.36), calls=%async_computation.7 | async-start | bytes 786432 | tf_op jit(solution)/shard_map/all_to_all | solution.py:255
  240.4 4.2 %collective-permute-done.6.ka_ref = bf16[768,512]{1,0:T(8,128)(2,1)} collective-permute-done((bf16[768,512]{1,0:T(8,128)(2,1)}, bf16[768,512]{1,0:T(8,128)(2,1)}, u32[]{:S(2)}, u32[]{:S(2)}) %collective-permute-start.6) | collective-permute-done | bytes 786464 | tf_op jit(solution)/shard_map/ppermute | solution.py:246
  244.6 6.2 %collective-permute-done.7.kc_ref = bf16[768,512]{1,0:T(8,128)(2,1)} collective-permute-done((bf16[768,512]{1,0:T(8,128)(2,1)}, bf16[768,512]{1,0:T(8,128)(2,1)}, u32[]{:S(2)}, u32[]{:S(2)}) %collective-permute-start.7) | collective-permute-done | bytes 786464 | tf_op jit(solution)/shard_map/ppermute | solution.py:245
  250.9 9.5 %far_attention.5.far_ref = bf16[792,256]{1,0:T(8,128)(2,1)} custom-call(s32[1]{0:T(128)} %bitcast.receives.active, bf16[768,256]{1,0:T(8,128)(2,1)} %slice.34.q_ref, bf16[768,512]{1,0:T(8,128)(2,1)} %collective-permute-done.6.ka_ref, bf16[768,512]{1,0:T(8,128)(2,1)} %collective-permute-done.5.kb_ref, bf16[768,512]{1,0:T(8,128)(2,1)} %collective-permute-done.7.kc_ref, ...), custom_call_target="tpu_custom_call" | custom-call | tf_op jit(solution)/shard_map/far_attention/pallas_call | solution.py:134
  260.4 4.3 %near_attention.5 = bf16[768,256]{1,0:T(8,128)(2,1)} custom-call(s32[1]{0:T(128)} %bitcast.receives.active, bf16[768,256]{1,0:T(8,128)(2,1)} %slice.34.q_ref, bf16[768,512]{1,0:T(8,128)(2,1)} %copy-done.5, bf16[792,256]{1,0:T(8,128)(2,1)} %far_attention.5.far_ref), custom_call_target="tpu_custom_call" | custom-call | tf_op jit(solution)/shard_map/near_attention/pallas_call | solution.py:193
  264.6 13.4 %all_to_all.42.refs_1_ = bf16[8,96,256]{2,1,0:T(8,128)(2,1)} all-to-all(bf16[8,96,256]{2,1,0:T(8,128)(2,1)} %bitcast.37), channel_id=1, replica_groups=mesh['head'=8,'ctx'=32] {'head'}, dimensions={0} | all-to-all | bytes 786432 | tf_op jit(solution)/shard_map/all_to_all | solution.py:255
  278.1 5.2 %unpack.1 = bf16[96,8192]{1,0:T(8,128)(2,1)} custom-call(bf16[8,96,256]{2,1,0:T(8,128)(2,1)} %copy-done.6, bf16[8,96,256]{2,1,0:T(8,128)(2,1)} %all_to_all.42.refs_1_, bf16[8,96,256]{2,1,0:T(8,128)(2,1)} %copy-done.7, bf16[8,96,256]{2,1,0:T(8,128)(2,1)} %copy-done.8), custom_call_target="tpu_custom_call" | custom-call | tf_op jit(solution)/shard_map/unpack/pallas_call | solution.py:120
  (75 shorter events, 23.3 us)
Async XLA Ops:
  6.9 22.0 %copy-start.9 = (bf16[8,96,768]{2,1,0:T(8,128)(2,1)S(1)}, bf16[8,96,768]{2,1,0:T(8,128)(2,1)}, u32[]{:S(2)}) copy-start(bf16[8,96,768]{2,1,0:T(8,128)(2,1)} %get-tuple-element.11) | copy-start | bytes 3538948
  49.4 20.8 %all-to-all-start.6 = ((bf16[8,96,768]{2,1,0:T(8,128)(2,1)}), bf16[8,96,768]{2,1,0:T(8,128)(2,1)S(1)}, u32[]{:S(2)}, u32[]{:S(2)}) async-start(bf16[8,96,768]{2,1,0:T(8,128)(2,1)} %get-tuple-element.12), calls=%async_computation.6 | async-start | bytes 2359296 | tf_op jit(solution)/shard_map/all_to_all | solution.py:240
  53.0 10.2 %copy-start.13 = (s32[3,1,6,6]{3,1,2,0:T(1,128)S(1)}, s32[3,1,6,6]{3,1,2,0:T(1,128)}, u32[]{:S(2)}) copy-start(s32[3,1,6,6]{3,1,2,0:T(1,128)} %param.8) | copy-start | bytes 1300
  53.1 17.2 %copy-start = (bf16[768,512]{1,0:T(8,128)(2,1)}, bf16[768,512]{1,0:T(8,128)(2,1)S(1)}, u32[]{:S(2)}) copy-start(bf16[768,512]{1,0:T(8,128)(2,1)S(1)} %slice.33.kb_ref.kv_ref) | copy-start | bytes 2359300
  53.1 35.3 %collective-permute-start.1 = (bf16[768,512]{1,0:T(8,128)(2,1)S(1)}, bf16[768,512]{1,0:T(8,128)(2,1)}, u32[]{:S(2)}, u32[]{:S(2)}) collective-permute-start(bf16[768,512]{1,0:T(8,128)(2,1)S(1)} %slice.33.kb_ref.kv_ref), channel_id=1, source_target_pairs={{1,0},{2,1},{3,2},{4,3},{5,4},{6,5},{7,6},{8,7},{9,8},{10,9},{11,1... | collective-permute-start | bytes 2359304 | tf_op jit(solution)/shard_map/ppermute | solution.py:251
  54.7 35.3 %collective-permute-start.2 = (bf16[768,512]{1,0:T(8,128)(2,1)S(1)}, bf16[768,512]{1,0:T(8,128)(2,1)}, u32[]{:S(2)}, u32[]{:S(2)}) collective-permute-start(bf16[768,512]{1,0:T(8,128)(2,1)S(1)} %slice.33.kb_ref.kv_ref), channel_id=1, source_target_pairs={{0,1},{1,2},{2,3},{3,4},{4,5},{5,6},{6,7},{7,8},{8,9},{9,10},{10,1... | collective-permute-start | bytes 2359304 | tf_op jit(solution)/shard_map/ppermute | solution.py:250
  57.0 29.8 %collective-permute-start = (bf16[768,256]{1,0:T(8,128)(2,1)}, bf16[768,256]{1,0:T(8,128)(2,1)}, u32[]{:S(2)}, u32[]{:S(2)}) collective-permute-start(bf16[768,256]{1,0:T(8,128)(2,1)} %slice.32.q_ref), channel_id=1, source_target_pairs={{15,31},{16,0},{17,1},{18,2},{19,3},{20,4},{21,5},{22,6},{23,7},{2... | collective-permute-start | bytes 1179656 | tf_op jit(solution)/shard_map/ppermute | solution.py:249
  63.3 17.0 %collective-permute-start.3 = (s32[3,6,6]{2,1,0:T(8,128)S(1)}, s32[3,6,6]{2,1,0:T(8,128)S(1)}, u32[]{:S(2)}, u32[]{:S(2)}) collective-permute-start(s32[3,6,6]{2,1,0:T(8,128)S(1)} %bitcast_select_fusion), channel_id=1, source_target_pairs={{15,31},{16,0},{17,1},{18,2},{19,3},{20,4},{21,5},{22,6},{23,7},{2... | collective-permute-start | bytes 1304 | tf_op jit(solution)/shard_map/ppermute | solution.py:235
  71.3 47.3 %all-to-all-start.2 = ((bf16[8,96,768]{2,1,0:T(8,128)(2,1)}), bf16[8,96,768]{2,1,0:T(8,128)(2,1)S(1)}, u32[]{:S(2)}, u32[]{:S(2)}) async-start(bf16[8,96,768]{2,1,0:T(8,128)(2,1)} %get-tuple-element.10), calls=%async_computation.2 | async-start | bytes 2359296 | tf_op jit(solution)/shard_map/all_to_all | solution.py:240
  80.4 6.3 %copy-start.4 = (bf16[8,96,768]{2,1,0:T(8,128)(2,1)S(1)}, bf16[8,96,768]{2,1,0:T(8,128)(2,1)}, u32[]{:S(2)}) copy-start(bf16[8,96,768]{2,1,0:T(8,128)(2,1)} %copy-done.3) | copy-start | bytes 3538948
  83.5 27.2 %copy-start.2 = (bf16[768,512]{1,0:T(8,128)(2,1)}, bf16[768,512]{1,0:T(8,128)(2,1)S(1)}, u32[]{:S(2)}) copy-start(bf16[768,512]{1,0:T(8,128)(2,1)S(1)} %slice.37.kb_ref.kv_ref) | copy-start | bytes 2359300
  83.5 35.2 %collective-permute-start.9 = (bf16[768,512]{1,0:T(8,128)(2,1)S(1)}, bf16[768,512]{1,0:T(8,128)(2,1)}, u32[]{:S(2)}, u32[]{:S(2)}) collective-permute-start(bf16[768,512]{1,0:T(8,128)(2,1)S(1)} %slice.37.kb_ref.kv_ref), channel_id=1, source_target_pairs={{1,0},{2,1},{3,2},{4,3},{5,4},{6,5},{7,6},{8,7},{9,8},{10,9},{11,1... | collective-permute-start | bytes 2359304 | tf_op jit(solution)/shard_map/ppermute | solution.py:251
  85.1 36.6 %collective-permute-start.10 = (bf16[768,512]{1,0:T(8,128)(2,1)S(1)}, bf16[768,512]{1,0:T(8,128)(2,1)}, u32[]{:S(2)}, u32[]{:S(2)}) collective-permute-start(bf16[768,512]{1,0:T(8,128)(2,1)S(1)} %slice.37.kb_ref.kv_ref), channel_id=1, source_target_pairs={{0,1},{1,2},{2,3},{3,4},{4,5},{5,6},{6,7},{7,8},{8,9},{9,10},{10,1... | collective-permute-start | bytes 2359304 | tf_op jit(solution)/shard_map/ppermute | solution.py:250
  86.7 24.0 %copy-start.1 = (bf16[768,512]{1,0:T(8,128)(2,1)}, bf16[768,512]{1,0:T(8,128)(2,1)S(1)}, u32[]{:S(2)}) copy-start(bf16[768,512]{1,0:T(8,128)(2,1)S(1)} %slice.39.kb_ref.kv_ref) | copy-start | bytes 2359300
  86.8 73.1 %collective-permute-start.13 = (bf16[768,512]{1,0:T(8,128)(2,1)S(1)}, bf16[768,512]{1,0:T(8,128)(2,1)}, u32[]{:S(2)}, u32[]{:S(2)}) collective-permute-start(bf16[768,512]{1,0:T(8,128)(2,1)S(1)} %slice.39.kb_ref.kv_ref), channel_id=1, source_target_pairs={{1,0},{2,1},{3,2},{4,3},{5,4},{6,5},{7,6},{8,7},{9,8},{10,9},{11,1... | collective-permute-start | bytes 2359304 | tf_op jit(solution)/shard_map/ppermute | solution.py:251
  88.4 71.5 %collective-permute-start.14 = (bf16[768,512]{1,0:T(8,128)(2,1)S(1)}, bf16[768,512]{1,0:T(8,128)(2,1)}, u32[]{:S(2)}, u32[]{:S(2)}) collective-permute-start(bf16[768,512]{1,0:T(8,128)(2,1)S(1)} %slice.39.kb_ref.kv_ref), channel_id=1, source_target_pairs={{0,1},{1,2},{2,3},{3,4},{4,5},{5,6},{6,7},{7,8},{8,9},{9,10},{10,1... | collective-permute-start | bytes 2359304 | tf_op jit(solution)/shard_map/ppermute | solution.py:250
  89.9 27.3 %collective-permute-start.8 = (bf16[768,256]{1,0:T(8,128)(2,1)}, bf16[768,256]{1,0:T(8,128)(2,1)S(1)}, u32[]{:S(2)}, u32[]{:S(2)}) collective-permute-start(bf16[768,256]{1,0:T(8,128)(2,1)} %slice.36.q_ref), channel_id=1, source_target_pairs={{15,31},{16,0},{17,1},{18,2},{19,3},{20,4},{21,5},{22,6},{23,7},{2... | collective-permute-start | bytes 1179656 | tf_op jit(solution)/shard_map/ppermute | solution.py:249
  117.3 33.3 %collective-permute-start.4 = (bf16[792,256]{1,0:T(8,128)(2,1)}, bf16[792,256]{1,0:T(8,128)(2,1)}, u32[]{:S(2)}, u32[]{:S(2)}) collective-permute-start(bf16[792,256]{1,0:T(8,128)(2,1)} %far_attention.4), channel_id=1, source_target_pairs={{31,15},{0,16},{1,17},{2,18},{3,19},{4,20},{5,21},{6,22},{7,23},{8... | collective-permute-start | bytes 1216520 | tf_op jit(solution)/shard_map/ppermute | solution.py:253
  118.6 16.6 %copy-start.5 = (bf16[768,512]{1,0:T(8,128)(2,1)}, bf16[768,512]{1,0:T(8,128)(2,1)S(1)}, u32[]{:S(2)}) copy-start(bf16[768,512]{1,0:T(8,128)(2,1)S(1)} %slice.35.kv_ref) | copy-start | bytes 2359300
  118.7 90.0 %collective-permute-start.5 = (bf16[768,512]{1,0:T(8,128)(2,1)S(1)}, bf16[768,512]{1,0:T(8,128)(2,1)}, u32[]{:S(2)}, u32[]{:S(2)}) collective-permute-start(bf16[768,512]{1,0:T(8,128)(2,1)S(1)} %slice.35.kv_ref), channel_id=1, source_target_pairs={{0,16},{1,17},{2,18},{3,19},{4,20},{5,21},{6,22},{7,23},{8,24},{9,... | collective-permute-start | bytes 2359304 | tf_op jit(solution)/shard_map/ppermute | solution.py:244
  121.7 38.1 %collective-permute-start.12 = (bf16[768,256]{1,0:T(8,128)(2,1)}, bf16[768,256]{1,0:T(8,128)(2,1)S(1)}, u32[]{:S(2)}, u32[]{:S(2)}) collective-permute-start(bf16[768,256]{1,0:T(8,128)(2,1)} %slice.38.q_ref), channel_id=1, source_target_pairs={{15,31},{16,0},{17,1},{18,2},{19,3},{20,4},{21,5},{22,6},{23,7},{2... | collective-permute-start | bytes 1179656 | tf_op jit(solution)/shard_map/ppermute | solution.py:249
  150.6 49.8 %collective-permute-start.11 = (bf16[792,256]{1,0:T(8,128)(2,1)}, bf16[792,256]{1,0:T(8,128)(2,1)}, u32[]{:S(2)}, u32[]{:S(2)}) collective-permute-start(bf16[792,256]{1,0:T(8,128)(2,1)} %far_attention.6), channel_id=1, source_target_pairs={{31,15},{0,16},{1,17},{2,18},{3,19},{4,20},{5,21},{6,22},{7,23},{8... | collective-permute-start | bytes 1216520 | tf_op jit(solution)/shard_map/ppermute | solution.py:253
  156.2 48.5 %all-to-all-start.1 = ((bf16[8,96,256]{2,1,0:T(8,128)(2,1)}), bf16[8,96,256]{2,1,0:T(8,128)(2,1)S(1)}, u32[]{:S(2)}, u32[]{:S(2)}) async-start(bf16[8,96,256]{2,1,0:T(8,128)(2,1)} %bitcast.35), calls=%async_computation.1 | async-start | bytes 786432 | tf_op jit(solution)/shard_map/all_to_all | solution.py:255
  163.9 64.9 %copy-start.14 = (s32[3,1,6,6]{3,1,2,0:T(1,128)S(1)}, s32[3,1,6,6]{3,1,2,0:T(1,128)}, u32[]{:S(2)}) copy-start(s32[3,1,6,6]{3,1,2,0:T(1,128)} %param.8) | copy-start | bytes 1300
  163.9 65.1 %collective-permute-start.15 = (bf16[792,256]{1,0:T(8,128)(2,1)}, bf16[792,256]{1,0:T(8,128)(2,1)S(1)}, u32[]{:S(2)}, u32[]{:S(2)}) collective-permute-start(bf16[792,256]{1,0:T(8,128)(2,1)} %far_attention.7), channel_id=1, source_target_pairs={{31,15},{0,16},{1,17},{2,18},{3,19},{4,20},{5,21},{6,22},{7,23},{8... | collective-permute-start | bytes 1216520 | tf_op jit(solution)/shard_map/ppermute | solution.py:253
  204.7 29.4 %copy-start.6 = (bf16[8,96,256]{2,1,0:T(8,128)(2,1)}, bf16[8,96,256]{2,1,0:T(8,128)(2,1)S(1)}, u32[]{:S(2)}) copy-start(bf16[8,96,256]{2,1,0:T(8,128)(2,1)S(1)} %all-to-all-done.1.refs_0_) | copy-start | bytes 1179652
  204.7 29.4 %all-to-all-start.5 = ((bf16[8,96,256]{2,1,0:T(8,128)(2,1)}), bf16[8,96,256]{2,1,0:T(8,128)(2,1)S(1)}, u32[]{:S(2)}, u32[]{:S(2)}) async-start(bf16[8,96,256]{2,1,0:T(8,128)(2,1)} %bitcast.34), calls=%async_computation.5 | async-start | bytes 786432 | tf_op jit(solution)/shard_map/all_to_all | solution.py:255
  208.6 36.0 %collective-permute-start.6 = (bf16[768,512]{1,0:T(8,128)(2,1)}, bf16[768,512]{1,0:T(8,128)(2,1)}, u32[]{:S(2)}, u32[]{:S(2)}) collective-permute-start(bf16[768,512]{1,0:T(8,128)(2,1)} %collective-permute-done.5.kb_ref), channel_id=1, source_target_pairs={{16,15},{17,16},{18,17},{19,18},{20,19},{21,20},{22,21},{23,22},{2... | collective-permute-start | bytes 2359304 | tf_op jit(solution)/shard_map/ppermute | solution.py:246
  226.9 24.0 %collective-permute-start.7 = (bf16[768,512]{1,0:T(8,128)(2,1)}, bf16[768,512]{1,0:T(8,128)(2,1)}, u32[]{:S(2)}, u32[]{:S(2)}) collective-permute-start(bf16[768,512]{1,0:T(8,128)(2,1)} %collective-permute-done.5.kb_ref), channel_id=1, source_target_pairs={{16,17},{17,18},{18,19},{19,20},{20,21},{21,22},{22,23},{23,24},{2... | collective-permute-start | bytes 2359304 | tf_op jit(solution)/shard_map/ppermute | solution.py:245
  234.1 26.3 %copy-start.7 = (bf16[8,96,256]{2,1,0:T(8,128)(2,1)}, bf16[8,96,256]{2,1,0:T(8,128)(2,1)S(1)}, u32[]{:S(2)}) copy-start(bf16[8,96,256]{2,1,0:T(8,128)(2,1)S(1)} %all-to-all-done.5.refs_2_) | copy-start | bytes 1179652
  234.1 30.5 %all-to-all-start.7 = ((bf16[8,96,256]{2,1,0:T(8,128)(2,1)}), bf16[8,96,256]{2,1,0:T(8,128)(2,1)S(1)}, u32[]{:S(2)}, u32[]{:S(2)}) async-start(bf16[8,96,256]{2,1,0:T(8,128)(2,1)} %bitcast.36), calls=%async_computation.7 | async-start | bytes 786432 | tf_op jit(solution)/shard_map/all_to_all | solution.py:255
  264.6 13.4 %copy-start.8 = (bf16[8,96,256]{2,1,0:T(8,128)(2,1)}, bf16[8,96,256]{2,1,0:T(8,128)(2,1)S(1)}, u32[]{:S(2)}) copy-start(bf16[8,96,256]{2,1,0:T(8,128)(2,1)S(1)} %all-to-all-done.7.refs_3_) | copy-start | bytes 1179652
  (5 other events, 7.0 us)

commit v4 on v3

--- a/solution.py
+++ b/solution.py
@@ -110,19 +110,22 @@
 
 def unpack_kernel(*refs):
     pieces, whole = refs[:-1], refs[-1]
-    cols = pieces[0].shape[2]
-    for n, piece in enumerate(pieces):
-        whole[:, n * cols : (n + 1) * cols] = piece[0]
+    groups, _, cols = pieces[0].shape
+    for g in range(groups):
+        for n, piece in enumerate(pieces):
+            start = (g * len(pieces) + n) * cols
+            whole[:, start : start + cols] = piece[g]
 
 
 def unpack(pieces, width):
     groups, rows, cols = pieces[0].shape
+    steps = 2
     return pl.pallas_call(
         unpack_kernel,
         out_shape=jax.ShapeDtypeStruct((rows, width), jnp.bfloat16),
-        grid=(groups,),
-        in_specs=[pl.BlockSpec((1, rows, cols), lambda g: (g, 0, 0))] * len(pieces),
-        out_specs=pl.BlockSpec((rows, width // groups), lambda g: (0, g)),
+        grid=(steps,),
+        in_specs=[pl.BlockSpec((groups // steps, rows, cols), lambda g: (g, 0, 0))] * len(pieces),
+        out_specs=pl.BlockSpec((rows, width // steps), lambda g: (0, g)),
         name="unpack",
     )(*pieces)
 

time: 285 us -> 282 us (0.989)
  no operation moved by 1% of the time
where the time goes in v4:
time: 282 us; the launch traced here: 280 us
  starting transfers between devices  88.7 us (31%)
  waiting for transfers between devices  78.6 us (28%)
  blocking collectives  55.9 us (20%)
  Pallas kernels  46.1 us (16%)
  local copies, waits for them, and re-layouts  10.7 us (4%)
    ppermute x3, waiting for transfers between devices, layer(): far_o = lax.ppermute(far_o, 'ctx', back)  50.5 us
    all_to_all x2, blocking collectives, layer(): lax.all_to_all(packed, 'head', split_axis=0, concat_axis=0, tiled=True)  42.5 us
    ppermute x3, starting transfers between devices, layer(): far_q = lax.ppermute(q, 'ctx', there)  33 us
    pallas_call x4, Pallas kernels, far_attention(): pl.pallas_call(far_kernel, out_shape=jax.ShapeDtypeStruct((C + TAIL, cols...  19.6 us
    ppermute x1, starting transfers between devices, layer(): after = lax.ppermute(shipped, 'ctx', pass_after)  18.2 us
    pallas_call x4, Pallas kernels, near_attention(): pl.pallas_call(near_kernel, out_shape=jax.ShapeDtypeStruct(q.shape, jnp.b...  17.1 us
    all_to_all x1, blocking collectives, layer(): lax.all_to_all(out.reshape(groups, tok_rows, cols), 'head', split_axis=0,...  13.4 us
    all_to_all x3, starting transfers between devices, layer(): lax.all_to_all(out.reshape(groups, tok_rows, cols), 'head', split_axis=0,...  12.4 us
  transfers between devices with their start and end apart: 21, of which 7 were waited for; matrix products, arithmetic and copies ran while one was open for 3% of the time, Pallas kernels for 13%

profile of v4, /device:TPU:192, one launch (start us, length us, event | category | flops | bytes accessed | tf_op | source)
XLA Modules:
  0.0 280.5 jit_solution(4514670693000327617)
XLA Ops:
  0.0 6.9 %pack.1 = (bf16[8,96,768]{2,1,0:T(8,128)(2,1)}, bf16[8,96,768]{2,1,0:T(8,128)(2,1)}, bf16[8,96,768]{2,1,0:T(8,128)(2,1)}, bf16[8,96,768]{2,1,0:T(8,128)(2,1)}) custom-call(bf16[96,8192]{1,0:T(8,128)(2,1)} %refs_0_.1, bf16[96,8192]{1,0:T(8,128)(2,1)} %refs_1_.1, bf16[96,8192]{1,0:T(8,128)(2,1)} %refs_2_.1), custom_call_target="tpu_custom_call" | custom-call | tf_op jit(solution)/shard_map/pack/pallas_call | solution.py:101
  6.9 22.0 %all_to_all.40 = bf16[8,96,768]{2,1,0:T(8,128)(2,1)S(1)} all-to-all(bf16[8,96,768]{2,1,0:T(8,128)(2,1)} %get-tuple-element.9), channel_id=1, replica_groups=mesh['head'=8,'ctx'=32] {'head'}, dimensions={0} | all-to-all | bytes 2359296 | tf_op jit(solution)/shard_map/all_to_all | solution.py:243
  28.9 20.5 %all_to_all.41 = bf16[8,96,768]{2,1,0:T(8,128)(2,1)} all-to-all(bf16[8,96,768]{2,1,0:T(8,128)(2,1)S(1)} %copy-done.9), channel_id=1, replica_groups=mesh['head'=8,'ctx'=32] {'head'}, dimensions={0} | all-to-all | bytes 2359296 | tf_op jit(solution)/shard_map/all_to_all | solution.py:243
  49.4 3.6 %all-to-all-start.6 = ((bf16[8,96,768]{2,1,0:T(8,128)(2,1)}), bf16[8,96,768]{2,1,0:T(8,128)(2,1)S(1)}, u32[]{:S(2)}, u32[]{:S(2)}) async-start(bf16[8,96,768]{2,1,0:T(8,128)(2,1)} %get-tuple-element.12), calls=%async_computation.6 | async-start | bytes 2359296 | tf_op jit(solution)/shard_map/all_to_all | solution.py:243
  57.0 6.2 %collective-permute-start = (bf16[768,256]{1,0:T(8,128)(2,1)}, bf16[768,256]{1,0:T(8,128)(2,1)}, u32[]{:S(2)}, u32[]{:S(2)}) collective-permute-start(bf16[768,256]{1,0:T(8,128)(2,1)} %slice.32.q_ref), channel_id=1, source_target_pairs={{15,31},{16,0},{17,1},{18,2},{19,3},{20,4},{21,5},{22,6},{23,7},{2... | collective-permute-start | bytes 1179656 | tf_op jit(solution)/shard_map/ppermute | solution.py:252
  64.6 5.6 %all-to-all-done.6 = bf16[8,96,768]{2,1,0:T(8,128)(2,1)S(1)} async-done(((bf16[8,96,768]{2,1,0:T(8,128)(2,1)}), bf16[8,96,768]{2,1,0:T(8,128)(2,1)S(1)}, u32[]{:S(2)}, u32[]{:S(2)}) %all-to-all-start.6) | async-done | bytes 1179680 | tf_op jit(solution)/shard_map/all_to_all | solution.py:243
  71.3 3.6 %all-to-all-start.2 = ((bf16[8,96,768]{2,1,0:T(8,128)(2,1)}), bf16[8,96,768]{2,1,0:T(8,128)(2,1)S(1)}, u32[]{:S(2)}, u32[]{:S(2)}) async-start(bf16[8,96,768]{2,1,0:T(8,128)(2,1)} %get-tuple-element.10), calls=%async_computation.2 | async-start | bytes 2359296 | tf_op jit(solution)/shard_map/all_to_all | solution.py:243
  74.8 5.4 %collective-permute-done.3 = s32[3,6,6]{2,1,0:T(8,128)S(1)} collective-permute-done((s32[3,6,6]{2,1,0:T(8,128)S(1)}, s32[3,6,6]{2,1,0:T(8,128)S(1)}, u32[]{:S(2)}, u32[]{:S(2)}) %collective-permute-start.3) | collective-permute-done | bytes 464 | tf_op jit(solution)/shard_map/ppermute | solution.py:238
  80.4 1.9 slice.36.q_ref
  89.9 16.7 %collective-permute-start.8 = (bf16[768,256]{1,0:T(8,128)(2,1)}, bf16[768,256]{1,0:T(8,128)(2,1)S(1)}, u32[]{:S(2)}, u32[]{:S(2)}) collective-permute-start(bf16[768,256]{1,0:T(8,128)(2,1)} %slice.36.q_ref), channel_id=1, source_target_pairs={{15,31},{16,0},{17,1},{18,2},{19,3},{20,4},{21,5},{22,6},{23,7},{2... | collective-permute-start | bytes 1179656 | tf_op jit(solution)/shard_map/ppermute | solution.py:252
  107.3 3.4 %far_attention.4 = bf16[792,256]{1,0:T(8,128)(2,1)} custom-call(s32[1]{0:T(128)} %bitcast.2.active, bf16[768,256]{1,0:T(8,128)(2,1)} %collective-permute-done.q_ref, bf16[768,512]{1,0:T(8,128)(2,1)} %collective-permute-done.1.ka_ref, bf16[768,512]{1,0:T(8,128)(2,1)} %copy-done, bf16[768,512]{1,0:T(8,128)(2,1)} %collective-permute-done.2.kc_ref, ...), custom_call_target="tpu_custom_call" | custom-call | tf_op jit(solution)/shard_map/far_attention/pallas_call | solution.py:137
  110.7 6.6 %collective-permute-done.8.q_ref = bf16[768,256]{1,0:T(8,128)(2,1)S(1)} collective-permute-done((bf16[768,256]{1,0:T(8,128)(2,1)}, bf16[768,256]{1,0:T(8,128)(2,1)S(1)}, u32[]{:S(2)}, u32[]{:S(2)}) %collective-permute-start.8) | collective-permute-done | bytes 393248 | tf_op jit(solution)/shard_map/ppermute | solution.py:252
  120.0 1.8 slice.38.q_ref
  121.7 10.1 %collective-permute-start.12 = (bf16[768,256]{1,0:T(8,128)(2,1)}, bf16[768,256]{1,0:T(8,128)(2,1)S(1)}, u32[]{:S(2)}, u32[]{:S(2)}) collective-permute-start(bf16[768,256]{1,0:T(8,128)(2,1)} %slice.38.q_ref), channel_id=1, source_target_pairs={{15,31},{16,0},{17,1},{18,2},{19,3},{20,4},{21,5},{22,6},{23,7},{2... | collective-permute-start | bytes 1179656 | tf_op jit(solution)/shard_map/ppermute | solution.py:252
  131.9 3.4 %far_attention.6 = bf16[792,256]{1,0:T(8,128)(2,1)} custom-call(s32[1]{0:T(128)} %bitcast.2.active, bf16[768,256]{1,0:T(8,128)(2,1)} %copy-done.12, bf16[768,512]{1,0:T(8,128)(2,1)} %collective-permute-done.9.ka_ref, bf16[768,512]{1,0:T(8,128)(2,1)} %copy-done.2, bf16[768,512]{1,0:T(8,128)(2,1)} %collective-permute-done.10.kc_ref, ...), custom_call_target="tpu_custom_call" | custom-call | tf_op jit(solution)/shard_map/far_attention/pallas_call | solution.py:137
  135.2 15.4 %collective-permute-done.4.far_ref = bf16[792,256]{1,0:T(8,128)(2,1)} collective-permute-done((bf16[792,256]{1,0:T(8,128)(2,1)}, bf16[792,256]{1,0:T(8,128)(2,1)}, u32[]{:S(2)}, u32[]{:S(2)}) %collective-permute-start.4) | collective-permute-done | bytes 405536 | tf_op jit(solution)/shard_map/ppermute | solution.py:256
  151.9 4.3 %near_attention.4 = bf16[768,256]{1,0:T(8,128)(2,1)} custom-call(s32[1]{0:T(128)} %bitcast.receives.active, bf16[768,256]{1,0:T(8,128)(2,1)} %slice.32.q_ref, bf16[768,512]{1,0:T(8,128)(2,1)} %copy-done, bf16[792,256]{1,0:T(8,128)(2,1)} %collective-permute-done.4.far_ref), custom_call_target="tpu_custom_call" | custom-call | tf_op jit(solution)/shard_map/near_attention/pallas_call | solution.py:196
  156.2 3.6 %all-to-all-start.1 = ((bf16[8,96,256]{2,1,0:T(8,128)(2,1)}), bf16[8,96,256]{2,1,0:T(8,128)(2,1)S(1)}, u32[]{:S(2)}, u32[]{:S(2)}) async-start(bf16[8,96,256]{2,1,0:T(8,128)(2,1)} %bitcast.35), calls=%async_computation.1 | async-start | bytes 786432 | tf_op jit(solution)/shard_map/all_to_all | solution.py:258
  160.6 3.4 %far_attention.7 = bf16[792,256]{1,0:T(8,128)(2,1)} custom-call(s32[1]{0:T(128)} %bitcast.2.active, bf16[768,256]{1,0:T(8,128)(2,1)} %copy-done.11, bf16[768,512]{1,0:T(8,128)(2,1)} %collective-permute-done.13.ka_ref, bf16[768,512]{1,0:T(8,128)(2,1)} %copy-done.1, bf16[768,512]{1,0:T(8,128)(2,1)} %collective-permute-done.14.kc_ref, ...), custom_call_target="tpu_custom_call" | custom-call | tf_op jit(solution)/shard_map/far_attention/pallas_call | solution.py:137
  165.3 35.1 %collective-permute-done.11.far_ref = bf16[792,256]{1,0:T(8,128)(2,1)} collective-permute-done((bf16[792,256]{1,0:T(8,128)(2,1)}, bf16[792,256]{1,0:T(8,128)(2,1)}, u32[]{:S(2)}, u32[]{:S(2)}) %collective-permute-start.11) | collective-permute-done | bytes 405536 | tf_op jit(solution)/shard_map/ppermute | solution.py:256
  200.4 4.3 %near_attention.6 = bf16[768,256]{1,0:T(8,128)(2,1)} custom-call(s32[1]{0:T(128)} %bitcast.receives.active, bf16[768,256]{1,0:T(8,128)(2,1)} %slice.36.q_ref, bf16[768,512]{1,0:T(8,128)(2,1)} %copy-done.2, bf16[792,256]{1,0:T(8,128)(2,1)} %collective-permute-done.11.far_ref), custom_call_target="tpu_custom_call" | custom-call | tf_op jit(solution)/shard_map/near_attention/pallas_call | solution.py:196
  204.7 3.9 %all-to-all-start.5 = ((bf16[8,96,256]{2,1,0:T(8,128)(2,1)}), bf16[8,96,256]{2,1,0:T(8,128)(2,1)S(1)}, u32[]{:S(2)}, u32[]{:S(2)}) async-start(bf16[8,96,256]{2,1,0:T(8,128)(2,1)} %bitcast.34), calls=%async_computation.5 | async-start | bytes 786432 | tf_op jit(solution)/shard_map/all_to_all | solution.py:258
  208.6 18.2 %collective-permute-start.6 = (bf16[768,512]{1,0:T(8,128)(2,1)}, bf16[768,512]{1,0:T(8,128)(2,1)}, u32[]{:S(2)}, u32[]{:S(2)}) collective-permute-start(bf16[768,512]{1,0:T(8,128)(2,1)} %collective-permute-done.5.kb_ref), channel_id=1, source_target_pairs={{16,15},{17,16},{18,17},{19,18},{20,19},{21,20},{22,21},{23,22},{2... | collective-permute-start | bytes 2359304 | tf_op jit(solution)/shard_map/ppermute | solution.py:249
  226.9 1.9 collective-permute-start.7
  229.8 4.3 %near_attention.7 = bf16[768,256]{1,0:T(8,128)(2,1)} custom-call(s32[1]{0:T(128)} %bitcast.receives.active, bf16[768,256]{1,0:T(8,128)(2,1)} %slice.38.q_ref, bf16[768,512]{1,0:T(8,128)(2,1)} %copy-done.1, bf16[792,256]{1,0:T(8,128)(2,1)} %copy-done.10), custom_call_target="tpu_custom_call" | custom-call | tf_op jit(solution)/shard_map/near_attention/pallas_call | solution.py:196
  234.1 4.8 %all-to-all-start.7 = ((bf16[8,96,256]{2,1,0:T(8,128)(2,1)}), bf16[8,96,256]{2,1,0:T(8,128)(2,1)S(1)}, u32[]{:S(2)}, u32[]{:S(2)}) async-start(bf16[8,96,256]{2,1,0:T(8,128)(2,1)} %bitcast.36), calls=%async_computation.7 | async-start | bytes 786432 | tf_op jit(solution)/shard_map/all_to_all | solution.py:258
  240.4 4.2 %collective-permute-done.6.ka_ref = bf16[768,512]{1,0:T(8,128)(2,1)} collective-permute-done((bf16[768,512]{1,0:T(8,128)(2,1)}, bf16[768,512]{1,0:T(8,128)(2,1)}, u32[]{:S(2)}, u32[]{:S(2)}) %collective-permute-start.6) | collective-permute-done | bytes 786464 | tf_op jit(solution)/shard_map/ppermute | solution.py:249
  244.6 6.2 %collective-permute-done.7.kc_ref = bf16[768,512]{1,0:T(8,128)(2,1)} collective-permute-done((bf16[768,512]{1,0:T(8,128)(2,1)}, bf16[768,512]{1,0:T(8,128)(2,1)}, u32[]{:S(2)}, u32[]{:S(2)}) %collective-permute-start.7) | collective-permute-done | bytes 786464 | tf_op jit(solution)/shard_map/ppermute | solution.py:248
  250.9 9.5 %far_attention.5.far_ref = bf16[792,256]{1,0:T(8,128)(2,1)} custom-call(s32[1]{0:T(128)} %bitcast.receives.active, bf16[768,256]{1,0:T(8,128)(2,1)} %slice.34.q_ref, bf16[768,512]{1,0:T(8,128)(2,1)} %collective-permute-done.6.ka_ref, bf16[768,512]{1,0:T(8,128)(2,1)} %collective-permute-done.5.kb_ref, bf16[768,512]{1,0:T(8,128)(2,1)} %collective-permute-done.7.kc_ref, ...), custom_call_target="tpu_custom_call" | custom-call | tf_op jit(solution)/shard_map/far_attention/pallas_call | solution.py:137
  260.4 4.3 %near_attention.5 = bf16[768,256]{1,0:T(8,128)(2,1)} custom-call(s32[1]{0:T(128)} %bitcast.receives.active, bf16[768,256]{1,0:T(8,128)(2,1)} %slice.34.q_ref, bf16[768,512]{1,0:T(8,128)(2,1)} %copy-done.5, bf16[792,256]{1,0:T(8,128)(2,1)} %far_attention.5.far_ref), custom_call_target="tpu_custom_call" | custom-call | tf_op jit(solution)/shard_map/near_attention/pallas_call | solution.py:196
  264.6 13.4 %all_to_all.42.refs_1_ = bf16[8,96,256]{2,1,0:T(8,128)(2,1)} all-to-all(bf16[8,96,256]{2,1,0:T(8,128)(2,1)} %bitcast.37), channel_id=1, replica_groups=mesh['head'=8,'ctx'=32] {'head'}, dimensions={0} | all-to-all | bytes 786432 | tf_op jit(solution)/shard_map/all_to_all | solution.py:258
  278.1 2.4 unpack.1
  (75 shorter events, 23.3 us)
Async XLA Ops:
  6.9 22.0 %copy-start.9 = (bf16[8,96,768]{2,1,0:T(8,128)(2,1)S(1)}, bf16[8,96,768]{2,1,0:T(8,128)(2,1)}, u32[]{:S(2)}) copy-start(bf16[8,96,768]{2,1,0:T(8,128)(2,1)} %get-tuple-element.11) | copy-start | bytes 3538948
  49.4 20.8 %all-to-all-start.6 = ((bf16[8,96,768]{2,1,0:T(8,128)(2,1)}), bf16[8,96,768]{2,1,0:T(8,128)(2,1)S(1)}, u32[]{:S(2)}, u32[]{:S(2)}) async-start(bf16[8,96,768]{2,1,0:T(8,128)(2,1)} %get-tuple-element.12), calls=%async_computation.6 | async-start | bytes 2359296 | tf_op jit(solution)/shard_map/all_to_all | solution.py:243
  53.0 10.2 %copy-start.13 = (s32[3,1,6,6]{3,1,2,0:T(1,128)S(1)}, s32[3,1,6,6]{3,1,2,0:T(1,128)}, u32[]{:S(2)}) copy-start(s32[3,1,6,6]{3,1,2,0:T(1,128)} %param.8) | copy-start | bytes 1300
  53.1 17.2 %copy-start = (bf16[768,512]{1,0:T(8,128)(2,1)}, bf16[768,512]{1,0:T(8,128)(2,1)S(1)}, u32[]{:S(2)}) copy-start(bf16[768,512]{1,0:T(8,128)(2,1)S(1)} %slice.33.kb_ref.kv_ref) | copy-start | bytes 2359300
  53.1 35.3 %collective-permute-start.1 = (bf16[768,512]{1,0:T(8,128)(2,1)S(1)}, bf16[768,512]{1,0:T(8,128)(2,1)}, u32[]{:S(2)}, u32[]{:S(2)}) collective-permute-start(bf16[768,512]{1,0:T(8,128)(2,1)S(1)} %slice.33.kb_ref.kv_ref), channel_id=1, source_target_pairs={{1,0},{2,1},{3,2},{4,3},{5,4},{6,5},{7,6},{8,7},{9,8},{10,9},{11,1... | collective-permute-start | bytes 2359304 | tf_op jit(solution)/shard_map/ppermute | solution.py:254
  54.7 35.3 %collective-permute-start.2 = (bf16[768,512]{1,0:T(8,128)(2,1)S(1)}, bf16[768,512]{1,0:T(8,128)(2,1)}, u32[]{:S(2)}, u32[]{:S(2)}) collective-permute-start(bf16[768,512]{1,0:T(8,128)(2,1)S(1)} %slice.33.kb_ref.kv_ref), channel_id=1, source_target_pairs={{0,1},{1,2},{2,3},{3,4},{4,5},{5,6},{6,7},{7,8},{8,9},{9,10},{10,1... | collective-permute-start | bytes 2359304 | tf_op jit(solution)/shard_map/ppermute | solution.py:253
  57.0 29.8 %collective-permute-start = (bf16[768,256]{1,0:T(8,128)(2,1)}, bf16[768,256]{1,0:T(8,128)(2,1)}, u32[]{:S(2)}, u32[]{:S(2)}) collective-permute-start(bf16[768,256]{1,0:T(8,128)(2,1)} %slice.32.q_ref), channel_id=1, source_target_pairs={{15,31},{16,0},{17,1},{18,2},{19,3},{20,4},{21,5},{22,6},{23,7},{2... | collective-permute-start | bytes 1179656 | tf_op jit(solution)/shard_map/ppermute | solution.py:252
  63.3 17.0 %collective-permute-start.3 = (s32[3,6,6]{2,1,0:T(8,128)S(1)}, s32[3,6,6]{2,1,0:T(8,128)S(1)}, u32[]{:S(2)}, u32[]{:S(2)}) collective-permute-start(s32[3,6,6]{2,1,0:T(8,128)S(1)} %bitcast_select_fusion), channel_id=1, source_target_pairs={{15,31},{16,0},{17,1},{18,2},{19,3},{20,4},{21,5},{22,6},{23,7},{2... | collective-permute-start | bytes 1304 | tf_op jit(solution)/shard_map/ppermute | solution.py:238
  71.3 47.3 %all-to-all-start.2 = ((bf16[8,96,768]{2,1,0:T(8,128)(2,1)}), bf16[8,96,768]{2,1,0:T(8,128)(2,1)S(1)}, u32[]{:S(2)}, u32[]{:S(2)}) async-start(bf16[8,96,768]{2,1,0:T(8,128)(2,1)} %get-tuple-element.10), calls=%async_computation.2 | async-start | bytes 2359296 | tf_op jit(solution)/shard_map/all_to_all | solution.py:243
  80.4 6.3 %copy-start.4 = (bf16[8,96,768]{2,1,0:T(8,128)(2,1)S(1)}, bf16[8,96,768]{2,1,0:T(8,128)(2,1)}, u32[]{:S(2)}) copy-start(bf16[8,96,768]{2,1,0:T(8,128)(2,1)} %copy-done.3) | copy-start | bytes 3538948
  83.5 27.2 %copy-start.2 = (bf16[768,512]{1,0:T(8,128)(2,1)}, bf16[768,512]{1,0:T(8,128)(2,1)S(1)}, u32[]{:S(2)}) copy-start(bf16[768,512]{1,0:T(8,128)(2,1)S(1)} %slice.37.kb_ref.kv_ref) | copy-start | bytes 2359300
  83.5 35.2 %collective-permute-start.9 = (bf16[768,512]{1,0:T(8,128)(2,1)S(1)}, bf16[768,512]{1,0:T(8,128)(2,1)}, u32[]{:S(2)}, u32[]{:S(2)}) collective-permute-start(bf16[768,512]{1,0:T(8,128)(2,1)S(1)} %slice.37.kb_ref.kv_ref), channel_id=1, source_target_pairs={{1,0},{2,1},{3,2},{4,3},{5,4},{6,5},{7,6},{8,7},{9,8},{10,9},{11,1... | collective-permute-start | bytes 2359304 | tf_op jit(solution)/shard_map/ppermute | solution.py:254
  85.1 36.6 %collective-permute-start.10 = (bf16[768,512]{1,0:T(8,128)(2,1)S(1)}, bf16[768,512]{1,0:T(8,128)(2,1)}, u32[]{:S(2)}, u32[]{:S(2)}) collective-permute-start(bf16[768,512]{1,0:T(8,128)(2,1)S(1)} %slice.37.kb_ref.kv_ref), channel_id=1, source_target_pairs={{0,1},{1,2},{2,3},{3,4},{4,5},{5,6},{6,7},{7,8},{8,9},{9,10},{10,1... | collective-permute-start | bytes 2359304 | tf_op jit(solution)/shard_map/ppermute | solution.py:253
  86.7 24.0 %copy-start.1 = (bf16[768,512]{1,0:T(8,128)(2,1)}, bf16[768,512]{1,0:T(8,128)(2,1)S(1)}, u32[]{:S(2)}) copy-start(bf16[768,512]{1,0:T(8,128)(2,1)S(1)} %slice.39.kb_ref.kv_ref) | copy-start | bytes 2359300
  86.8 73.1 %collective-permute-start.13 = (bf16[768,512]{1,0:T(8,128)(2,1)S(1)}, bf16[768,512]{1,0:T(8,128)(2,1)}, u32[]{:S(2)}, u32[]{:S(2)}) collective-permute-start(bf16[768,512]{1,0:T(8,128)(2,1)S(1)} %slice.39.kb_ref.kv_ref), channel_id=1, source_target_pairs={{1,0},{2,1},{3,2},{4,3},{5,4},{6,5},{7,6},{8,7},{9,8},{10,9},{11,1... | collective-permute-start | bytes 2359304 | tf_op jit(solution)/shard_map/ppermute | solution.py:254
  88.4 71.5 %collective-permute-start.14 = (bf16[768,512]{1,0:T(8,128)(2,1)S(1)}, bf16[768,512]{1,0:T(8,128)(2,1)}, u32[]{:S(2)}, u32[]{:S(2)}) collective-permute-start(bf16[768,512]{1,0:T(8,128)(2,1)S(1)} %slice.39.kb_ref.kv_ref), channel_id=1, source_target_pairs={{0,1},{1,2},{2,3},{3,4},{4,5},{5,6},{6,7},{7,8},{8,9},{9,10},{10,1... | collective-permute-start | bytes 2359304 | tf_op jit(solution)/shard_map/ppermute | solution.py:253
  89.9 27.3 %collective-permute-start.8 = (bf16[768,256]{1,0:T(8,128)(2,1)}, bf16[768,256]{1,0:T(8,128)(2,1)S(1)}, u32[]{:S(2)}, u32[]{:S(2)}) collective-permute-start(bf16[768,256]{1,0:T(8,128)(2,1)} %slice.36.q_ref), channel_id=1, source_target_pairs={{15,31},{16,0},{17,1},{18,2},{19,3},{20,4},{21,5},{22,6},{23,7},{2... | collective-permute-start | bytes 1179656 | tf_op jit(solution)/shard_map/ppermute | solution.py:252
  117.3 33.3 %collective-permute-start.4 = (bf16[792,256]{1,0:T(8,128)(2,1)}, bf16[792,256]{1,0:T(8,128)(2,1)}, u32[]{:S(2)}, u32[]{:S(2)}) collective-permute-start(bf16[792,256]{1,0:T(8,128)(2,1)} %far_attention.4), channel_id=1, source_target_pairs={{31,15},{0,16},{1,17},{2,18},{3,19},{4,20},{5,21},{6,22},{7,23},{8... | collective-permute-start | bytes 1216520 | tf_op jit(solution)/shard_map/ppermute | solution.py:256
  118.6 16.6 %copy-start.5 = (bf16[768,512]{1,0:T(8,128)(2,1)}, bf16[768,512]{1,0:T(8,128)(2,1)S(1)}, u32[]{:S(2)}) copy-start(bf16[768,512]{1,0:T(8,128)(2,1)S(1)} %slice.35.kv_ref) | copy-start | bytes 2359300
  118.7 90.0 %collective-permute-start.5 = (bf16[768,512]{1,0:T(8,128)(2,1)S(1)}, bf16[768,512]{1,0:T(8,128)(2,1)}, u32[]{:S(2)}, u32[]{:S(2)}) collective-permute-start(bf16[768,512]{1,0:T(8,128)(2,1)S(1)} %slice.35.kv_ref), channel_id=1, source_target_pairs={{0,16},{1,17},{2,18},{3,19},{4,20},{5,21},{6,22},{7,23},{8,24},{9,... | collective-permute-start | bytes 2359304 | tf_op jit(solution)/shard_map/ppermute | solution.py:247
  121.7 38.1 %collective-permute-start.12 = (bf16[768,256]{1,0:T(8,128)(2,1)}, bf16[768,256]{1,0:T(8,128)(2,1)S(1)}, u32[]{:S(2)}, u32[]{:S(2)}) collective-permute-start(bf16[768,256]{1,0:T(8,128)(2,1)} %slice.38.q_ref), channel_id=1, source_target_pairs={{15,31},{16,0},{17,1},{18,2},{19,3},{20,4},{21,5},{22,6},{23,7},{2... | collective-permute-start | bytes 1179656 | tf_op jit(solution)/shard_map/ppermute | solution.py:252
  150.6 49.8 %collective-permute-start.11 = (bf16[792,256]{1,0:T(8,128)(2,1)}, bf16[792,256]{1,0:T(8,128)(2,1)}, u32[]{:S(2)}, u32[]{:S(2)}) collective-permute-start(bf16[792,256]{1,0:T(8,128)(2,1)} %far_attention.6), channel_id=1, source_target_pairs={{31,15},{0,16},{1,17},{2,18},{3,19},{4,20},{5,21},{6,22},{7,23},{8... | collective-permute-start | bytes 1216520 | tf_op jit(solution)/shard_map/ppermute | solution.py:256
  156.2 48.5 %all-to-all-start.1 = ((bf16[8,96,256]{2,1,0:T(8,128)(2,1)}), bf16[8,96,256]{2,1,0:T(8,128)(2,1)S(1)}, u32[]{:S(2)}, u32[]{:S(2)}) async-start(bf16[8,96,256]{2,1,0:T(8,128)(2,1)} %bitcast.35), calls=%async_computation.1 | async-start | bytes 786432 | tf_op jit(solution)/shard_map/all_to_all | solution.py:258
  163.9 64.9 %copy-start.14 = (s32[3,1,6,6]{3,1,2,0:T(1,128)S(1)}, s32[3,1,6,6]{3,1,2,0:T(1,128)}, u32[]{:S(2)}) copy-start(s32[3,1,6,6]{3,1,2,0:T(1,128)} %param.8) | copy-start | bytes 1300
  163.9 65.1 %collective-permute-start.15 = (bf16[792,256]{1,0:T(8,128)(2,1)}, bf16[792,256]{1,0:T(8,128)(2,1)S(1)}, u32[]{:S(2)}, u32[]{:S(2)}) collective-permute-start(bf16[792,256]{1,0:T(8,128)(2,1)} %far_attention.7), channel_id=1, source_target_pairs={{31,15},{0,16},{1,17},{2,18},{3,19},{4,20},{5,21},{6,22},{7,23},{8... | collective-permute-start | bytes 1216520 | tf_op jit(solution)/shard_map/ppermute | solution.py:256
  204.7 29.4 %copy-start.6 = (bf16[8,96,256]{2,1,0:T(8,128)(2,1)}, bf16[8,96,256]{2,1,0:T(8,128)(2,1)S(1)}, u32[]{:S(2)}) copy-start(bf16[8,96,256]{2,1,0:T(8,128)(2,1)S(1)} %all-to-all-done.1.refs_0_) | copy-start | bytes 1179652
  204.7 29.4 %all-to-all-start.5 = ((bf16[8,96,256]{2,1,0:T(8,128)(2,1)}), bf16[8,96,256]{2,1,0:T(8,128)(2,1)S(1)}, u32[]{:S(2)}, u32[]{:S(2)}) async-start(bf16[8,96,256]{2,1,0:T(8,128)(2,1)} %bitcast.34), calls=%async_computation.5 | async-start | bytes 786432 | tf_op jit(solution)/shard_map/all_to_all | solution.py:258
  208.6 36.0 %collective-permute-start.6 = (bf16[768,512]{1,0:T(8,128)(2,1)}, bf16[768,512]{1,0:T(8,128)(2,1)}, u32[]{:S(2)}, u32[]{:S(2)}) collective-permute-start(bf16[768,512]{1,0:T(8,128)(2,1)} %collective-permute-done.5.kb_ref), channel_id=1, source_target_pairs={{16,15},{17,16},{18,17},{19,18},{20,19},{21,20},{22,21},{23,22},{2... | collective-permute-start | bytes 2359304 | tf_op jit(solution)/shard_map/ppermute | solution.py:249
  226.9 24.0 %collective-permute-start.7 = (bf16[768,512]{1,0:T(8,128)(2,1)}, bf16[768,512]{1,0:T(8,128)(2,1)}, u32[]{:S(2)}, u32[]{:S(2)}) collective-permute-start(bf16[768,512]{1,0:T(8,128)(2,1)} %collective-permute-done.5.kb_ref), channel_id=1, source_target_pairs={{16,17},{17,18},{18,19},{19,20},{20,21},{21,22},{22,23},{23,24},{2... | collective-permute-start | bytes 2359304 | tf_op jit(solution)/shard_map/ppermute | solution.py:248
  234.1 26.3 %copy-start.7 = (bf16[8,96,256]{2,1,0:T(8,128)(2,1)}, bf16[8,96,256]{2,1,0:T(8,128)(2,1)S(1)}, u32[]{:S(2)}) copy-start(bf16[8,96,256]{2,1,0:T(8,128)(2,1)S(1)} %all-to-all-done.5.refs_2_) | copy-start | bytes 1179652
  234.1 30.5 %all-to-all-start.7 = ((bf16[8,96,256]{2,1,0:T(8,128)(2,1)}), bf16[8,96,256]{2,1,0:T(8,128)(2,1)S(1)}, u32[]{:S(2)}, u32[]{:S(2)}) async-start(bf16[8,96,256]{2,1,0:T(8,128)(2,1)} %bitcast.36), calls=%async_computation.7 | async-start | bytes 786432 | tf_op jit(solution)/shard_map/all_to_all | solution.py:258
  264.6 13.4 %copy-start.8 = (bf16[8,96,256]{2,1,0:T(8,128)(2,1)}, bf16[8,96,256]{2,1,0:T(8,128)(2,1)S(1)}, u32[]{:S(2)}) copy-start(bf16[8,96,256]{2,1,0:T(8,128)(2,1)S(1)} %all-to-all-done.7.refs_3_) | copy-start | bytes 1179652
  (5 other events, 7.0 us)
